TPU v7x, 256 devices: a whole 4x4x8 slice. The times are simulated.
256 devices in a mesh: space: 16 (over z, core), tracer: 4 (over x), month: 4 (over y).
Axes of the slice: x: 4, y: 4, z: 8, core: 2. Of those that a mesh axis runs over, the one named last changes fastest.
Arguments:
- state: float32 [32, 16, 128, 512], P('tracer', 'month', 'space'), may hold values from -20 to 20
- coefficients: bfloat16 [4, 27, 16, 128, 512], P('month', None, None, 'space'), may hold values from 0 to 1, as said below
- rates: float32 [32], P('tracer'), may hold values from 0.05 to 0.5
- land_mask: int32 [128, 512], P('space'), may hold values 0 or 1
- wet_levels: int32 [128, 512], P('space'), may hold values from 1 to 16
- basis: float32 [4, 32, 16, 128, 512], P(None, 'tracer', 'month', 'space'), may hold values from -20 to 20
Outputs:
- residual: float32 [32, 16, 128, 512], P('tracer', 'month', 'space')
- next_basis: float32 [32, 16, 128, 512], P('tracer', 'month', 'space')
- krylov: float32 [6], replicated
Inputs may be any that keep to these rules, and one draw needn't show every extreme that they name: `coefficients`: the 27 weights of a cell in a month are non-negative and sum to one.
All inputs are finite; a program needn't handle non-finite values. No bound on the sum of `land_mask` on one device may be relied on, other than what follows from the above.
Results may differ from a plain program's by a relative error of at most 0.0011.
Values may be sent and summed in bfloat16 or wider, within the bound.
No kernel may reach another device: no remote copies, remote signals or barrier semaphores. Data moves between devices by JAX's collectives and lax.ppermute only.
A program may use at most 64 MiB of HBM per device.

v0:
```python
import functools

import jax
import jax.numpy as jnp
from jax import lax
from jax.experimental import pallas as pl
from jax.experimental.pallas import tpu as pltpu
from jax.sharding import PartitionSpec as P


F32 = jnp.float32
BF16 = jnp.bfloat16
TAPS = [(dl, di) for dl in (-1, 0, 1) for di in (-1, 0, 1)]


VMEM_LIMIT = 20 * 2**20


def call(body, outs, cost, scratch=(), in_specs=None):
    return pl.pallas_call(
        body,
        out_shape=[jax.ShapeDtypeStruct(s, d) for s, d in outs],
        scratch_shapes=list(scratch),
        cost_estimate=pl.CostEstimate(flops=cost, transcendentals=0, bytes_accessed=cost // 8),
        compiler_params=pltpu.CompilerParams(vmem_limit_bytes=VMEM_LIMIT),
        **({} if in_specs is None else {"in_specs": in_specs}),
    )


def keep_of(axis):
    place = lax.axis_index(axis)
    return [jnp.where(place > 0, 1.0, 0.0), jnp.where(place < lax.axis_size(axis) - 1, 1.0, 0.0)]


def reader(levels, columns, inner_ref, outer_ref, sides_ref):
    def get(f, l, i):
        if i in (0, columns - 1):
            return sides_ref[f, l, int(i > 0)]
        if l in (0, levels - 1):
            return outer_ref[f, int(l > 0), i]
        return inner_ref[f, l - 1, i]

    return get


def init_body(levels, columns, rates_ref, land_ref, depth_ref, state_ref, basis_ref, *outs):
    inner_ref, outer_ref, sides_ref, wet_ref, rate_ref, lev_lo, lev_hi, lon_lo, lon_hi, last_ref, sem = outs
    fetch = pltpu.make_async_copy(basis_ref.at[basis_ref.shape[0] - 1], last_ref, sem)
    fetch.start()
    tracer = lax.broadcasted_iota(jnp.int32, rate_ref.shape, 0)
    rate = jnp.zeros(rate_ref.shape, F32)
    for n in range(rate_ref.shape[0]):
        rate = jnp.where(tracer == n, rates_ref[n], rate)
    rate_ref[...] = rate
    for l in range(levels):
        ocean = (land_ref[...] == 1) & (lax.axis_index("month") * levels + l < depth_ref[...])
        wet_ref[l] = jnp.where(ocean, 1.0, 0.0).astype(F32)
    for f, ref in enumerate((state_ref, last_ref)):
        if f:
            fetch.wait()
        for l in range(levels):
            rows = pltpu.einshape("tix->itx", ref[:, l])
            for i in range(columns):
                row = rows[i] * wet_ref[l, pl.ds(i, 1), :]
                short = row.astype(BF16)
                if i in (0, columns - 1):
                    sides_ref[f, l, int(i > 0)] = row
                    (lon_hi if i else lon_lo)[f, l] = short
                elif l in (0, levels - 1):
                    outer_ref[f, int(l > 0), i] = row
                else:
                    inner_ref[f, l - 1, i] = row
                if l in (0, levels - 1):
                    (lev_hi if l else lev_lo)[f, i] = short


def combine(sums):
    n = sums[1].shape[1]
    return sums[1] + pltpu.roll(sums[2], n - 1, 1) + pltpu.roll(sums[0], 1, 1)


def tap_sums(taps):
    acc = [[None] * 3, [None] * 3]
    for weights, rows in taps:
        for dj in range(3):
            for f in range(2):
                term = weights[dj] * rows[f]
                acc[f][dj] = term if acc[f][dj] is None else acc[f][dj] + term
    return combine(acc[0]), combine(acc[1])


def prepare_body(month, months, *refs):
    sources, wf_ref = refs[:-1], refs[-1]
    n_parts = lax.axis_size("tracer")
    size = sources[0].shape[3]
    taps, levels, columns, lat = wf_ref.shape
    me = lax.axis_index("month")
    tests = [me == month] + [me < month] * (month > 0) + [me > month] * (month < months - 1)
    for n, test in enumerate(tests):

        @pl.when(test)
        def _(parts=sources[n * n_parts : (n + 1) * n_parts]):
            for n, ref in enumerate(parts):
                place = lax.rem(lax.axis_index("tracer") - n + n_parts, n_parts)
                lanes = pl.ds(pl.multiple_of(place * size, size), size)

                def spread_part(k, carry, ref=ref, lanes=lanes):
                    for l in range(levels):
                        wf_ref[k, l, :, lanes] = ref[k, l].astype(F32)
                    return carry

                lax.fori_loop(0, taps, spread_part, 0, unroll=3)

    lane = lax.broadcasted_iota(jnp.int32, (columns, lat), 1)

    def move(k, carry):
        for l in range(levels):
            wf_ref[3 * k + 2, l] = jnp.where(lane == 0, 0.0, pltpu.roll(wf_ref[3 * k + 2, l], 1, 1))
            wf_ref[3 * k, l] = jnp.where(lane == lat - 1, 0.0, pltpu.roll(wf_ref[3 * k, l], lat - 1, 1))
        return carry

    lax.fori_loop(0, taps // 3, move, 0, unroll=3)


def part_body(levels, columns, mine, outer, wf_ref, inner_ref, outer_ref, sides_ref, rate_ref, wet_ref, *rest):
    if outer:
        below_ref, above_ref, out_ref = rest
    else:
        (out_ref,) = rest
    get = reader(levels, columns, inner_ref, outer_ref, sides_ref)
    keep = keep_of("month")
    rate = rate_ref[...]

    def rows_at(l, i):
        if l < 0:
            return [below_ref[f, i].astype(F32) * keep[0] for f in range(2)]
        if l >= levels:
            return [above_ref[f, i].astype(F32) * keep[1] for f in range(2)]
        return [get(f, l, i) for f in range(2)]

    for n, l in enumerate(mine):
        for i in range(columns):
            taps = []
            for dl, di in TAPS:
                if 0 <= i + di < columns:
                    first = 9 * (dl + 1) + 3 * (di + 1)
                    weights = [wf_ref[first + dj, l, pl.ds(i, 1), :] for dj in range(3)]
                    taps.append((weights, rows_at(l + dl, i + di)))
            ac, at = tap_sums(taps)
            c, t = rows_at(l, i)
            square = c * c
            inverse = 1.0 / (1.0 + square)
            part = rate * square * inverse
            ac = ac - part * c
            at = at - part * inverse * (3.0 + square) * t
            if 0 < i < columns - 1:
                wet = wet_ref[l, pl.ds(i, 1), :]
                ac, at = ac * wet, at * wet
            out_ref[0, n, i] = ac
            out_ref[1, n, i] = at


def side_rows(levels, columns, inner_ref, outer_ref, wf_ref, left_ref, right_ref, wet_ref):
    keep_lev, keep_lon = keep_of("month"), keep_of("space")
    for l in range(levels):
        edge = l in (0, levels - 1)
        n = int(l > 0) if edge else l - 1
        own = outer_ref if edge else inner_ref
        for side, i in ((0, 0), (1, columns - 1)):
            halo = (left_ref, right_ref)[side]
            taps = []
            for d in range(3):
                keep = keep_lon[side]
                if not 0 <= l + d - 1 < levels:
                    keep = keep * keep_lev[int(l + d > levels)]
                weights = [wf_ref[9 * d + 6 * side + dj, l, pl.ds(i, 1), :] for dj in range(3)]
                taps.append((weights, [halo[f, l + d].astype(F32) * keep for f in range(2)]))
            sums = tap_sums(taps)
            wet = wet_ref[l, pl.ds(i, 1), :]
            yield l, side, i, [(own[f, n, i] + sums[f]) * wet for f in range(2)]


def side_body(levels, columns, *refs):
    sides_ref, lev_lo, lev_hi, lon_lo, lon_hi = refs[6:]
    outer_ref = refs[1]
    for l, side, i, rows in side_rows(levels, columns, *refs[:6]):
        for f in range(2):
            short = rows[f].astype(BF16)
            sides_ref[f, l, side] = rows[f]
            (lon_hi if side else lon_lo)[f, l] = short
            if l in (0, levels - 1):
                (lev_hi if l else lev_lo)[f, i] = short
    for f in range(2):
        for i in range(1, columns - 1):
            lev_lo[f, i] = outer_ref[f, 0, i].astype(BF16)
            lev_hi[f, i] = outer_ref[f, 1, i].astype(BF16)


def pack_body(columns, after_ref, below_ref, above_ref, lo_ref, hi_ref, left_out, right_out):
    levels = lo_ref.shape[1]
    for out, own, i in ((left_out, lo_ref, 0), (right_out, hi_ref, columns - 1)):
        for f in range(2):
            out[f, 0] = below_ref[f, i]
            out[f, levels + 1] = above_ref[f, i]
            for l in range(levels):
                out[f, l + 1] = own[f, l]


def lanes_of(values, first):
    lane = lax.broadcasted_iota(jnp.int32, (1, 128), 1)
    total = jnp.zeros((1, 128), F32)
    for n, v in enumerate(values):
        total = jnp.where(lane == first + n, v, total)
    return total


def gram_body(basis_ref, out_ref):
    count = basis_ref.shape[0]
    pairs = [(k, m) for k in range(count) for m in range(k, count)]

    def step(n, acc):
        rows = pl.ds(pl.multiple_of(n * 8, 8), 8)
        b = [basis_ref[k, rows, :] for k in range(count)]
        return tuple(a + b[k] * b[m] for a, (k, m) in zip(acc, pairs))

    zero = jnp.zeros((8, basis_ref.shape[2]), F32)
    acc = lax.fori_loop(0, basis_ref.shape[1] // 8, step, (zero,) * len(pairs))
    out_ref[...] = lanes_of([jnp.sum(a) for a in acc], 6)


def last_body(levels, columns, *refs):
    state_ref, basis_ref, gram_ref, res_ref, prod_ref, out_ref = refs[6:12]
    fields = refs[12:]
    inner_ref, outer_ref = refs[:2]
    sides = {}
    for l, side, i, rows in side_rows(levels, columns, *refs[:6]):
        sides[l, i] = rows
    for l in range(levels):
        for f in range(2):
            own = [sides[l, i][f] if i in (0, columns - 1)
                   else outer_ref[f, int(l > 0), i] if l in (0, levels - 1) else inner_ref[f, l - 1, i]
                   for i in range(columns)]
            fields[f][:, l] = pltpu.einshape("itx->tix", jnp.stack(own))
    count = basis_ref.shape[0]

    def step(n, acc):
        for l in range(levels):
            b = [basis_ref[k, n, l] for k in range(count)]
            residual = fields[0][n, l] - state_ref[n, l]
            product = fields[1][n, l] - b[count - 1]
            res_ref[n, l] = residual
            prod_ref[n, l] = product
            terms = [x * product for x in b] + [product * product, residual * residual]
            acc = tuple(a + x for a, x in zip(acc, terms))
        return acc

    zero = jnp.zeros(fields[0].shape[2:], F32)
    acc = lax.fori_loop(0, fields[0].shape[0], step, (zero,) * (count + 2))
    row = gram_ref[...] + lanes_of([jnp.sum(a) for a in acc], 0)
    for n in range(out_ref.shape[0]):
        out_ref[n] = row


def finish_body(cells, rows_ref, prod_ref, basis_ref, rem_ref, next_ref, krylov_ref, sure_ref):
    count = basis_ref.shape[0]
    means = rows_ref[0]
    for n in range(1, rows_ref.shape[0]):
        means = means + rows_ref[n]
    means = means / cells
    lane = lax.broadcasted_iota(jnp.int32, (1, 128), 1)

    def pick(n):
        return jnp.sum(jnp.where(lane == n, means, 0.0), axis=1, keepdims=True)

    coef = [pick(k) for k in range(count)]
    cross = sum(2.0 * c * c for c in coef)
    gram = 0.0
    place = count + 2
    for k in range(count):
        for m in range(k, count):
            gram = gram + (1.0 if k == m else 2.0) * coef[k] * coef[m] * pick(place)
            place += 1
    square = pick(count)
    expanded = square - cross + gram
    sure = jnp.where(expanded > 0.01 * (square + cross + gram), 1.0, 0.0)
    norm = jnp.sqrt(jnp.maximum(expanded, 0.0) + 1e-06)
    rms = jnp.sqrt(pick(count + 1) + 1e-06)
    krylov = jnp.where(lane == count, norm, jnp.where(lane == count + 1, rms, means))
    krylov_ref[...] = krylov[:, : count + 2]
    sure_ref[...] = sure
    inverse = 1.0 / norm

    def step(n, carry):
        rows = pl.ds(pl.multiple_of(n * 8, 8), 8)
        rem = coef[0] * basis_ref[0, rows, :]
        for k in range(1, count):
            rem = rem + coef[k] * basis_ref[k, rows, :]
        rem = prod_ref[rows, :] - rem
        rem_ref[rows, :] = rem
        next_ref[rows, :] = rem * inverse
        return carry

    lax.fori_loop(0, prod_ref.shape[0] // 8, step, 0)


def spread(x, axes):
    return lax.all_to_all(x, axes, 0, 0, tiled=True)


def copies(x, count):
    return jnp.broadcast_to(x[None], (count,) + x.shape)


def shifted(x, axis, by):
    size = lax.axis_size(axis)
    return lax.ppermute(x, axis, [(n, (n + by) % size) for n in range(size)])


def after(x, *others):
    return lax.optimization_barrier((x, *others))[0]


def extract_body(coef_ref, *refs):
    outs, sem = refs[:-1], refs[-1]
    levels, part = outs[0].shape[1], outs[0].shape[3]
    place = pl.ds(pl.multiple_of(lax.axis_index("tracer") * part, part), part)
    fetches = []
    for k, out in enumerate(outs):
        level = pl.ds(lax.rem(lax.axis_index("month") + k, len(outs)) * levels, levels)
        fetches.append(pltpu.make_async_copy(coef_ref.at[0, :, level, :, place], out, sem.at[k]))
        fetches[-1].start()
    for fetch in fetches:
        fetch.wait()


def month_parts(coefficients, levels):
    taps, _, columns, lat = coefficients.shape[1:]
    n_tracer, n_month = lax.axis_size("tracer"), lax.axis_size("month")
    own = call(
        extract_body,
        [((taps, levels, columns, lat // n_tracer), BF16)] * n_month,
        10**6,
        scratch=[pltpu.SemaphoreType.DMA((n_month,))],
        in_specs=[pl.BlockSpec(memory_space=pltpu.HBM)],
    )(pltpu.with_memory_space_constraint(coefficients, pltpu.HBM))
    return [own[0]] + [shifted(own[k], "month", k) for k in range(1, n_month)]


def select_body(turn, *refs):
    found, out = refs[:-1], refs[-1]
    me = lax.axis_index("month")
    month = jnp.where(turn < me, turn, turn + 1)
    place = lax.rem(me - month + len(found), len(found))
    for k, ref in enumerate(found):

        @pl.when(place == k)
        def _(ref=ref):
            out[...] = ref[...]


def of_turn(found, turn):
    return call(functools.partial(select_body, turn), [(found[0].shape, BF16)], 10**5)(*found)[0]


def one_step(state, coefficients, rates, land_mask, wet_levels, basis):
    tracers, levels, columns, lat = state.shape
    count = basis.shape[0]
    n_space, n_month, n_tracer = lax.axis_size("space"), lax.axis_size("month"), lax.axis_size("tracer")
    flat = (tracers * levels * columns, lat)
    basis_rows = basis.reshape((count,) + flat)
    found = month_parts(coefficients, levels)

    row = (tracers, lat)
    inner, outer = (2, levels - 2, columns) + row, (2, 2, columns) + row
    sides, lev, lon = (2, levels, 2) + row, (2, columns) + row, (2, levels) + row
    messages = [(lev, BF16)] * 2 + [(lon, BF16)] * 2
    vmem, smem = pl.BlockSpec(memory_space=pltpu.VMEM), pl.BlockSpec(memory_space=pltpu.SMEM)
    anywhere = pl.BlockSpec(memory_space=pl.ANY)
    field_a, field_b, field_s, wet, rate, *sent = call(
        functools.partial(init_body, levels, columns),
        [(inner, F32), (outer, F32), (sides, F32), ((levels, columns, lat), F32), (row, F32)] + messages,
        2 * 10**6,
        in_specs=[smem] + [vmem] * 3 + [anywhere],
        scratch=[pltpu.VMEM(state.shape, F32), pltpu.SemaphoreType.DMA],
    )(rates, land_mask, wet_levels, state, basis)
    (gram,) = call(gram_body, [((1, 128), F32)], 2 * 10**6)(basis_rows)

    def fetched(part):
        return [part] + [shifted(part, "tracer", k) for k in range(1, n_tracer)]

    def prepared(own, turns, month):
        sources = own + (turns[month - 1] if month else []) + (turns[month] if month < steps - 1 else [])
        return call(
            functools.partial(prepare_body, month, steps), [((27, levels, columns, lat), F32)], 2 * 10**6
        )(*sources)[0]

    inner_levels, outer_levels = list(range(1, levels - 1)), [0, levels - 1]
    steps = coefficients.shape[0] * n_month
    halos = shifted(sent[1], "month", 1), shifted(sent[0], "month", -1)
    own = fetched(found[0])
    turns = [fetched(after(of_turn(found, 0), gram))]
    found = lax.optimization_barrier((found, halos))[0]
    turns.append(fetched(of_turn(found, 1)))
    for month in range(steps):
        weights = prepared(own, turns, month) if month < 2 else next_weights
        lev_lo, lev_hi, lon_lo, lon_hi = sent
        below, above = halos if month == 0 else (shifted(lev_hi, "month", 1), shifted(lev_lo, "month", -1))
        args = (weights, field_a, field_b, field_s, rate, wet)

        def part(mine, shape, is_outer, *more):
            return call(
                functools.partial(part_body, levels, columns, mine, is_outer),
                [(shape, F32)],
                10**7,
            )(*args, *more)[0]

        new_a = part(inner_levels, inner, False)
        left, right = call(
            functools.partial(pack_body, columns),
            [((2, levels + 2) + row, BF16)] * 2,
            10**5,
            in_specs=[anywhere] + [vmem] * 4,
        )(new_a if month else wet, below, above, lon_lo, lon_hi)
        left, right = shifted(right, "space", 1), shifted(left, "space", -1)
        if month == 0:
            found = lax.optimization_barrier((found, left, right))[0]
            turns += [fetched(of_turn(found, turn)) for turn in range(2, steps - 1)]
        elif month < steps - 1:
            next_weights = prepared(own, turns, month + 1)
            left, right, next_weights = lax.optimization_barrier((left, right, next_weights))
        new_b = part(outer_levels, outer, True, below, above)
        field_a, field_b = new_a, new_b
        ends = (new_a, new_b, weights, left, right, wet)
        if month < steps - 1:
            field_s, *sent = call(
                functools.partial(side_body, levels, columns), [(sides, F32)] + messages, 2 * 10**6,
            )(*ends)

    residual, product, tiles = call(
        functools.partial(last_body, levels, columns),
        [(state.shape, F32)] * 2 + [((n_space * n_tracer, 1, 128), F32)],
        4 * 10**6,
        scratch=[pltpu.VMEM(state.shape, F32)] * 2,
    )(*ends, state, basis, gram)

    def total(tiles):
        part = jnp.sum(spread(tiles, ("space", "tracer")), axis=0)
        return spread(copies(part, n_month), "month")

    cells = float(state.size * n_space * n_tracer * n_month)
    remainder, next_basis, krylov, sure = call(
        functools.partial(finish_body, cells), [(flat, F32)] * 2 + [((1, count + 2), F32), ((1, 1), F32)], 2 * 10**6
    )(total(tiles), product.reshape(flat), basis_rows)

    def direct(remainder, next_basis, krylov):
        own = jnp.broadcast_to(jnp.sum(remainder * remainder), (n_space * n_tracer, 1, 128))
        norm = jnp.sqrt(jnp.sum(total(own), axis=0)[0, 0] / cells + 1e-06)
        return remainder / norm, jnp.where(jnp.arange(count + 2) == count, norm, krylov)

    next_basis, krylov = lax.cond(
        sure[0, 0] > 0.5, lambda r, n, k: (n, k), direct, remainder, next_basis, krylov
    )
    return residual, next_basis.reshape(state.shape), krylov.reshape(count + 2)


def solution(mesh):
    return jax.shard_map(
        one_step,
        mesh=mesh,
        in_specs=(
            P("tracer", "month", "space", None),
            P("month", None, None, "space", None),
            P("tracer"),
            P("space", None),
            P("space", None),
            P(None, "tracer", "month", "space", None),
        ),
        out_specs=(P("tracer", "month", "space", None), P("tracer", "month", "space", None), P()),
        check_vma=False,
    )
```

profile of v0, /device:TPU:1, one launch (start us, length us, event | category | flops | bytes accessed | tf_op | source)
XLA Modules:
  0.0 125.3 jit_solution(15019518749445239499)
XLA Ops:
  0.7 1.5 %shard_map.85 = (bf16[27,4,8,128]{3,2,1,0:T(8,128)(2,1)S(1)}, bf16[27,4,8,128]{3,2,1,0:T(8,128)(2,1)S(1)}, bf16[27,4,8,128]{3,2,1,0:T(8,128)(2,1)S(1)}, bf16[27,4,8,128]{3,2,1,0:T(8,128)(2,1)S(1)}) custom-call(bf16[1,27,16,8,512]{4,3,2,1,0:T(8,128)(2,1)} %coef_ref.1), custom_call_target="tpu_custom_call" | custom-call | flops 1000000 | bytes 125000 | tf_op jit(solution)/shard_map/pallas_call | solution.py:339
  2.2 2.2 %collective-permute-start.3 = (bf16[27,4,8,128]{3,2,1,0:T(8,128)(2,1)S(1)}, bf16[27,4,8,128]{3,2,1,0:T(8,128)(2,1)S(1)}, u32[]{:S(2)}, u32[]{:S(2)}) collective-permute-start(bf16[27,4,8,128]{3,2,1,0:T(8,128)(2,1)S(1)} %get-tuple-element.80), channel_id=1, source_target_pairs={{0,1},{1,2},{2,3},{3,0},{4,5},{5,6},{6,7},{7,4},{8,9},{9,10},{10,1... | collective-permute-start | bytes 663560 | tf_op jit(solution)/shard_map/ppermute | solution.py:316
  4.4 2.6 %collective-permute-start.4 = (bf16[27,4,8,128]{3,2,1,0:T(8,128)(2,1)S(1)}, bf16[27,4,8,128]{3,2,1,0:T(8,128)(2,1)S(1)}, u32[]{:S(2)}, u32[]{:S(2)}) collective-permute-start(bf16[27,4,8,128]{3,2,1,0:T(8,128)(2,1)S(1)} %get-tuple-element.81), channel_id=1, source_target_pairs={{0,2},{1,3},{2,0},{3,1},{4,6},{5,7},{6,4},{7,5},{8,10},{9,11},{10,... | collective-permute-start | bytes 663560 | tf_op jit(solution)/shard_map/ppermute | solution.py:316
  7.0 1.1 collective-permute-start.5
  8.1 0.8 shard_map.88
  8.9 0.5 collective-permute-start.9
  9.4 2.5 %collective-permute-start.2 = (bf16[27,4,8,128]{3,2,1,0:T(8,128)(2,1)S(1)}, bf16[27,4,8,128]{3,2,1,0:T(8,128)(2,1)S(1)}, u32[]{:S(2)}, u32[]{:S(2)}) collective-permute-start(bf16[27,4,8,128]{3,2,1,0:T(8,128)(2,1)S(1)} %get-tuple-element.106.refs_0_), channel_id=1, source_target_pairs={{0,12},{4,0},{8,4},{12,8},{1,13},{5,1},{9,5},{13,9},{2,14},{6,2},{... | collective-permute-start | bytes 663560 | tf_op jit(solution)/shard_map/ppermute | solution.py:316
  11.9 2.3 %collective-permute-start.10 = (bf16[2,8,8,512]{3,2,1,0:T(8,128)(2,1)S(1)}, bf16[2,8,8,512]{3,2,1,0:T(8,128)(2,1)S(1)}, u32[]{:S(2)}, u32[]{:S(2)}) collective-permute-start(bf16[2,8,8,512]{3,2,1,0:T(8,128)(2,1)S(1)} %get-tuple-element.85), channel_id=1, source_target_pairs={{0,3},{1,0},{2,1},{3,2},{4,7},{5,4},{6,5},{7,6},{8,11},{9,8},{10,9... | collective-permute-start | bytes 393224 | tf_op jit(solution)/shard_map/ppermute | solution.py:316
  14.2 1.0 shard_map.87.refs_8_
  15.2 1.5 %collective-permute-done.4.refs_2_ = bf16[27,4,8,128]{3,2,1,0:T(8,128)(2,1)S(1)} collective-permute-done((bf16[27,4,8,128]{3,2,1,0:T(8,128)(2,1)S(1)}, bf16[27,4,8,128]{3,2,1,0:T(8,128)(2,1)S(1)}, u32[]{:S(2)}, u32[]{:S(2)}) %collective-permute-start.4) | collective-permute-done | bytes 221216 | tf_op jit(solution)/shard_map/ppermute | solution.py:316
  16.6 2.7 %collective-permute-start.1 = (bf16[27,4,8,128]{3,2,1,0:T(8,128)(2,1)S(1)}, bf16[27,4,8,128]{3,2,1,0:T(8,128)(2,1)S(1)}, u32[]{:S(2)}, u32[]{:S(2)}) collective-permute-start(bf16[27,4,8,128]{3,2,1,0:T(8,128)(2,1)S(1)} %get-tuple-element.106.refs_0_), channel_id=1, source_target_pairs={{0,8},{4,12},{8,0},{12,4},{1,9},{5,13},{9,1},{13,5},{2,10},{6,14},... | collective-permute-start | bytes 663560 | tf_op jit(solution)/shard_map/ppermute | solution.py:316
  19.4 0.0 collective-permute-done.5.refs_3_
  19.4 0.3 collective-permute-start
  19.7 2.4 %collective-permute-start.8 = (bf16[27,4,8,128]{3,2,1,0:T(8,128)(2,1)S(1)}, bf16[27,4,8,128]{3,2,1,0:T(8,128)(2,1)S(1)}, u32[]{:S(2)}, u32[]{:S(2)}) collective-permute-start(bf16[27,4,8,128]{3,2,1,0:T(8,128)(2,1)S(1)} %shard_map.86.refs_4_), channel_id=1, source_target_pairs={{0,12},{4,0},{8,4},{12,8},{1,13},{5,1},{9,5},{13,9},{2,14},{6,2},{... | collective-permute-start | bytes 663560 | tf_op jit(solution)/shard_map/ppermute | solution.py:316
  22.2 0.0 collective-permute-done.10.rest_1_.above_ref
  22.2 0.1 collective-permute-start.7
  22.3 0.6 collective-permute-start.6
  22.9 0.0 collective-permute-done.1.refs_2_
  22.9 2.5 %collective-permute-start.13 = (bf16[27,4,8,128]{3,2,1,0:T(8,128)(2,1)S(1)}, bf16[27,4,8,128]{3,2,1,0:T(8,128)(2,1)S(1)}, u32[]{:S(2)}, u32[]{:S(2)}) collective-permute-start(bf16[27,4,8,128]{3,2,1,0:T(8,128)(2,1)S(1)} %shard_map.89.refs_8_.refs_4_), channel_id=1, source_target_pairs={{0,12},{4,0},{8,4},{12,8},{1,13},{5,1},{9,5},{13,9},{2,14},{6,2},{... | collective-permute-start | bytes 663560 | tf_op jit(solution)/shard_map/ppermute | solution.py:316
  25.4 4.1 %collective-permute-done.refs_1_ = bf16[27,4,8,128]{3,2,1,0:T(8,128)(2,1)S(1)} collective-permute-done((bf16[27,4,8,128]{3,2,1,0:T(8,128)(2,1)S(1)}, bf16[27,4,8,128]{3,2,1,0:T(8,128)(2,1)S(1)}, u32[]{:S(2)}, u32[]{:S(2)}) %collective-permute-start) | collective-permute-done | bytes 221216 | tf_op jit(solution)/shard_map/ppermute | solution.py:316
  29.5 2.9 %collective-permute-start.12 = (bf16[27,4,8,128]{3,2,1,0:T(8,128)(2,1)S(1)}, bf16[27,4,8,128]{3,2,1,0:T(8,128)(2,1)S(1)}, u32[]{:S(2)}, u32[]{:S(2)}) collective-permute-start(bf16[27,4,8,128]{3,2,1,0:T(8,128)(2,1)S(1)} %shard_map.89.refs_8_.refs_4_), channel_id=1, source_target_pairs={{0,8},{4,12},{8,0},{12,4},{1,9},{5,13},{9,1},{13,5},{2,10},{6,14},... | collective-permute-start | bytes 663560 | tf_op jit(solution)/shard_map/ppermute | solution.py:316
  32.4 7.8 %collective-permute-start.14 = (bf16[2,6,8,512]{3,2,1,0:T(8,128)(2,1)S(1)}, bf16[2,6,8,512]{3,2,1,0:T(8,128)(2,1)S(1)}, u32[]{:S(2)}, u32[]{:S(2)}) collective-permute-start(bf16[2,6,8,512]{3,2,1,0:T(8,128)(2,1)S(1)} %get-tuple-element.97), channel_id=1, source_target_pairs={{0,16},{16,32},{32,48},{48,64},{64,80},{80,96},{96,112},{112,128},... | collective-permute-start | bytes 294920 | tf_op jit(solution)/shard_map/ppermute | solution.py:316
  40.2 5.7 %collective-permute-start.15 = (bf16[2,6,8,512]{3,2,1,0:T(8,128)(2,1)S(1)}, bf16[2,6,8,512]{3,2,1,0:T(8,128)(2,1)S(1)}, u32[]{:S(2)}, u32[]{:S(2)}) collective-permute-start(bf16[2,6,8,512]{3,2,1,0:T(8,128)(2,1)S(1)} %get-tuple-element.98), channel_id=1, source_target_pairs={{0,240},{16,0},{32,16},{48,32},{64,48},{80,64},{96,80},{112,96},{1... | collective-permute-start | bytes 294920 | tf_op jit(solution)/shard_map/ppermute | solution.py:316
  45.9 0.9 shard_map.91.wf_ref.refs_2_
  46.9 1.6 %shard_map.92.refs_0_.inner_ref = f32[2,2,8,8,512]{4,3,2,1,0:T(8,128)S(1)} custom-call(f32[27,4,8,512]{3,2,1,0:T(8,128)S(1)} %shard_map.91.wf_ref.refs_2_, f32[2,2,8,8,512]{4,3,2,1,0:T(8,128)S(1)} %get-tuple-element.90.inner_ref, f32[2,2,8,8,512]{4,3,2,1,0:T(8,128)S(1)} %get-tuple-element.91.outer_ref, f32[2,4,2,8,512]{4,3,2,1,0:T(8,128)S(1)} %get-tuple-element.92.sides_ref, ...), custom_call_target="tpu_custom_call" | custom-call | flops 10000000 | bytes 1250000 | tf_op jit(solution)/shard_map/pallas_call | solution.py:411
  48.5 1.6 %shard_map.93.refs_1_.outer_ref = f32[2,2,8,8,512]{4,3,2,1,0:T(8,128)S(1)} custom-call(f32[27,4,8,512]{3,2,1,0:T(8,128)S(1)} %shard_map.91.wf_ref.refs_2_, f32[2,2,8,8,512]{4,3,2,1,0:T(8,128)S(1)} %get-tuple-element.90.inner_ref, f32[2,2,8,8,512]{4,3,2,1,0:T(8,128)S(1)} %get-tuple-element.91.outer_ref, f32[2,4,2,8,512]{4,3,2,1,0:T(8,128)S(1)} %get-tuple-element.92.sides_ref, ...), custom_call_target="tpu_custom_call" | custom-call | flops 10000000 | bytes 1250000 | tf_op jit(solution)/shard_map/pallas_call | solution.py:411
  50.2 0.3 shard_map.95
  50.5 0.1 collective-permute-start.16
  50.6 2.7 %collective-permute-start.17 = (bf16[2,8,8,512]{3,2,1,0:T(8,128)(2,1)S(1)}, bf16[2,8,8,512]{3,2,1,0:T(8,128)(2,1)S(1)}, u32[]{:S(2)}, u32[]{:S(2)}) collective-permute-start(bf16[2,8,8,512]{3,2,1,0:T(8,128)(2,1)S(1)} %get-tuple-element.101), channel_id=1, source_target_pairs={{0,3},{1,0},{2,1},{3,2},{4,7},{5,4},{6,5},{7,6},{8,11},{9,8},{10,9... | collective-permute-start | bytes 393224 | tf_op jit(solution)/shard_map/ppermute | solution.py:316
  53.3 0.1 collective-permute-start.22
  53.4 0.5 collective-permute-start.21
  53.8 1.1 collective-permute-start.20
  54.9 0.8 shard_map.90.wf_ref.refs_2_
  55.7 1.5 %shard_map.96.after_ref.refs_0_.inner_ref = f32[2,2,8,8,512]{4,3,2,1,0:T(8,128)S(1)} custom-call(f32[27,4,8,512]{3,2,1,0:T(8,128)S(1)} %shard_map.90.wf_ref.refs_2_, f32[2,2,8,8,512]{4,3,2,1,0:T(8,128)S(1)} %shard_map.92.refs_0_.inner_ref, f32[2,2,8,8,512]{4,3,2,1,0:T(8,128)S(1)} %shard_map.93.refs_1_.outer_ref, ...), custom_call_target="tpu_custom_call" | custom-call | flops 10000000 | bytes 1250000 | tf_op jit(solution)/shard_map/pallas_call | solution.py:411
  57.2 2.7 %collective-permute-start.18 = (bf16[2,6,8,512]{3,2,1,0:T(8,128)(2,1)S(1)}, bf16[2,6,8,512]{3,2,1,0:T(8,128)(2,1)S(1)}, u32[]{:S(2)}, u32[]{:S(2)}) collective-permute-start(bf16[2,6,8,512]{3,2,1,0:T(8,128)(2,1)S(1)} %get-tuple-element.104), channel_id=1, source_target_pairs={{0,16},{16,32},{32,48},{48,64},{64,80},{80,96},{96,112},{112,128},... | collective-permute-start | bytes 294920 | tf_op jit(solution)/shard_map/ppermute | solution.py:316
  59.9 1.5 %collective-permute-done.21.refs_10_.refs_6_ = bf16[27,4,8,128]{3,2,1,0:T(8,128)(2,1)S(1)} collective-permute-done((bf16[27,4,8,128]{3,2,1,0:T(8,128)(2,1)S(1)}, bf16[27,4,8,128]{3,2,1,0:T(8,128)(2,1)S(1)}, u32[]{:S(2)}, u32[]{:S(2)}) %collective-permute-start.21) | collective-permute-done | bytes 221216 | tf_op jit(solution)/shard_map/ppermute | solution.py:316
  61.4 5.6 %collective-permute-done.20.refs_9_.refs_5_ = bf16[27,4,8,128]{3,2,1,0:T(8,128)(2,1)S(1)} collective-permute-done((bf16[27,4,8,128]{3,2,1,0:T(8,128)(2,1)S(1)}, bf16[27,4,8,128]{3,2,1,0:T(8,128)(2,1)S(1)}, u32[]{:S(2)}, u32[]{:S(2)}) %collective-permute-start.20) | collective-permute-done | bytes 221216 | tf_op jit(solution)/shard_map/ppermute | solution.py:316
  67.1 0.8 shard_map.99.wf_ref.refs_2_
  67.8 1.5 %shard_map.100.refs_1_.outer_ref = f32[2,2,8,8,512]{4,3,2,1,0:T(8,128)S(1)} custom-call(f32[27,4,8,512]{3,2,1,0:T(8,128)S(1)} %shard_map.90.wf_ref.refs_2_, f32[2,2,8,8,512]{4,3,2,1,0:T(8,128)S(1)} %shard_map.92.refs_0_.inner_ref, f32[2,2,8,8,512]{4,3,2,1,0:T(8,128)S(1)} %shard_map.93.refs_1_.outer_ref, ...), custom_call_target="tpu_custom_call" | custom-call | flops 10000000 | bytes 1250000 | tf_op jit(solution)/shard_map/pallas_call | solution.py:411
  69.4 0.3 shard_map.101
  69.7 0.1 collective-permute-start.23
  69.8 2.7 %collective-permute-start.24 = (bf16[2,8,8,512]{3,2,1,0:T(8,128)(2,1)S(1)}, bf16[2,8,8,512]{3,2,1,0:T(8,128)(2,1)S(1)}, u32[]{:S(2)}, u32[]{:S(2)}) collective-permute-start(bf16[2,8,8,512]{3,2,1,0:T(8,128)(2,1)S(1)} %get-tuple-element.115), channel_id=1, source_target_pairs={{0,3},{1,0},{2,1},{3,2},{4,7},{5,4},{6,5},{7,6},{8,11},{9,8},{10,9... | collective-permute-start | bytes 393224 | tf_op jit(solution)/shard_map/ppermute | solution.py:316
  72.5 1.5 %shard_map.102.after_ref.refs_0_.inner_ref = f32[2,2,8,8,512]{4,3,2,1,0:T(8,128)S(1)} custom-call(f32[27,4,8,512]{3,2,1,0:T(8,128)S(1)} %shard_map.99.wf_ref.refs_2_, f32[2,2,8,8,512]{4,3,2,1,0:T(8,128)S(1)} %shard_map.96.after_ref.refs_0_.inner_ref, f32[2,2,8,8,512]{4,3,2,1,0:T(8,128)S(1)} %shard_map.100.refs_1_.outer_ref, ...), custom_call_target="tpu_custom_call" | custom-call | flops 10000000 | bytes 1250000 | tf_op jit(solution)/shard_map/pallas_call | solution.py:411
  74.0 1.6 %collective-permute-done.23.below_ref.rest_0_ = bf16[2,8,8,512]{3,2,1,0:T(8,128)(2,1)S(1)} collective-permute-done((bf16[2,8,8,512]{3,2,1,0:T(8,128)(2,1)S(1)}, bf16[2,8,8,512]{3,2,1,0:T(8,128)(2,1)S(1)}, u32[]{:S(2)}, u32[]{:S(2)}) %collective-permute-start.23) | collective-permute-done | bytes 131104 | tf_op jit(solution)/shard_map/ppermute | solution.py:316
  75.6 2.9 %collective-permute-start.25 = (bf16[2,6,8,512]{3,2,1,0:T(8,128)(2,1)S(1)}, bf16[2,6,8,512]{3,2,1,0:T(8,128)(2,1)S(1)}, u32[]{:S(2)}, u32[]{:S(2)}) collective-permute-start(bf16[2,6,8,512]{3,2,1,0:T(8,128)(2,1)S(1)} %get-tuple-element.118), channel_id=1, source_target_pairs={{0,16},{16,32},{32,48},{48,64},{64,80},{80,96},{96,112},{112,128},... | collective-permute-start | bytes 294920 | tf_op jit(solution)/shard_map/ppermute | solution.py:316
  78.5 0.8 shard_map.104.wf_ref.refs_2_
  79.2 1.5 %shard_map.105.refs_1_.outer_ref = f32[2,2,8,8,512]{4,3,2,1,0:T(8,128)S(1)} custom-call(f32[27,4,8,512]{3,2,1,0:T(8,128)S(1)} %shard_map.99.wf_ref.refs_2_, f32[2,2,8,8,512]{4,3,2,1,0:T(8,128)S(1)} %shard_map.96.after_ref.refs_0_.inner_ref, f32[2,2,8,8,512]{4,3,2,1,0:T(8,128)S(1)} %shard_map.100.refs_1_.outer_ref, ...), custom_call_target="tpu_custom_call" | custom-call | flops 10000000 | bytes 1250000 | tf_op jit(solution)/shard_map/pallas_call | solution.py:411
  80.8 2.0 %collective-permute-done.26.refs_4_ = bf16[2,6,8,512]{3,2,1,0:T(8,128)(2,1)S(1)} collective-permute-done((bf16[2,6,8,512]{3,2,1,0:T(8,128)(2,1)S(1)}, bf16[2,6,8,512]{3,2,1,0:T(8,128)(2,1)S(1)}, u32[]{:S(2)}, u32[]{:S(2)}) %collective-permute-start.26) | collective-permute-done | bytes 98336 | tf_op jit(solution)/shard_map/ppermute | solution.py:316
  82.8 0.3 shard_map.106
  83.1 0.1 collective-permute-start.27
  83.2 2.8 %collective-permute-start.28 = (bf16[2,8,8,512]{3,2,1,0:T(8,128)(2,1)S(1)}, bf16[2,8,8,512]{3,2,1,0:T(8,128)(2,1)S(1)}, u32[]{:S(2)}, u32[]{:S(2)}) collective-permute-start(bf16[2,8,8,512]{3,2,1,0:T(8,128)(2,1)S(1)} %get-tuple-element.125), channel_id=1, source_target_pairs={{0,3},{1,0},{2,1},{3,2},{4,7},{5,4},{6,5},{7,6},{8,11},{9,8},{10,9... | collective-permute-start | bytes 393224 | tf_op jit(solution)/shard_map/ppermute | solution.py:316
  85.9 1.5 %shard_map.107.after_ref.refs_0_ = f32[2,2,8,8,512]{4,3,2,1,0:T(8,128)S(1)} custom-call(f32[27,4,8,512]{3,2,1,0:T(8,128)S(1)} %shard_map.104.wf_ref.refs_2_, f32[2,2,8,8,512]{4,3,2,1,0:T(8,128)S(1)} %shard_map.102.after_ref.refs_0_.inner_ref, f32[2,2,8,8,512]{4,3,2,1,0:T(8,128)S(1)} %shard_map.105.refs_1_.outer_ref, ...), custom_call_target="tpu_custom_call" | custom-call | flops 10000000 | bytes 1250000 | tf_op jit(solution)/shard_map/pallas_call | solution.py:411
  87.5 0.7 collective-permute-done.27.rest_0_.below_ref
  88.2 1.3 %collective-permute-start.29 = (bf16[2,6,8,512]{3,2,1,0:T(8,128)(2,1)S(1)}, bf16[2,6,8,512]{3,2,1,0:T(8,128)(2,1)S(1)}, u32[]{:S(2)}, u32[]{:S(2)}) collective-permute-start(bf16[2,6,8,512]{3,2,1,0:T(8,128)(2,1)S(1)} %get-tuple-element.128), channel_id=1, source_target_pairs={{0,16},{16,32},{32,48},{48,64},{64,80},{80,96},{96,112},{112,128},... | collective-permute-start | bytes 294920 | tf_op jit(solution)/shard_map/ppermute | solution.py:316
  89.5 1.0 collective-permute-start.30
  90.5 1.6 %shard_map.108.refs_1_ = f32[2,2,8,8,512]{4,3,2,1,0:T(8,128)S(1)} custom-call(f32[27,4,8,512]{3,2,1,0:T(8,128)S(1)} %shard_map.104.wf_ref.refs_2_, f32[2,2,8,8,512]{4,3,2,1,0:T(8,128)S(1)} %shard_map.102.after_ref.refs_0_.inner_ref, f32[2,2,8,8,512]{4,3,2,1,0:T(8,128)S(1)} %shard_map.105.refs_1_.outer_ref, ...), custom_call_target="tpu_custom_call" | custom-call | flops 10000000 | bytes 1250000 | tf_op jit(solution)/shard_map/pallas_call | solution.py:411
  92.1 1.5 %collective-permute-done.30.refs_4_ = bf16[2,6,8,512]{3,2,1,0:T(8,128)(2,1)S(1)} collective-permute-done((bf16[2,6,8,512]{3,2,1,0:T(8,128)(2,1)S(1)}, bf16[2,6,8,512]{3,2,1,0:T(8,128)(2,1)S(1)}, u32[]{:S(2)}, u32[]{:S(2)}) %collective-permute-start.30) | collective-permute-done | bytes 98336 | tf_op jit(solution)/shard_map/ppermute | solution.py:316
  93.6 1.6 %shard_map.110 = (f32[8,4,8,512]{3,2,1,0:T(8,128)}, f32[8,4,8,512]{3,2,1,0:T(8,128)S(1)}, f32[64,1,128]{2,1,0:T(1,128)S(1)}) custom-call(f32[2,2,8,8,512]{4,3,2,1,0:T(8,128)S(1)} %shard_map.107.after_ref.refs_0_, f32[2,2,8,8,512]{4,3,2,1,0:T(8,128)S(1)} %shard_map.108.refs_1_, f32[27,4,8,512]{3,2,1,0:T(8,128)S(1)} %shard_map.104.wf_ref.refs_2_, ...), custom_call_target="tpu_custom_call" | custom-call | flops 4000000 | bytes 500000 | tf_op jit(solution)/shard_map/pallas_call | solution.py:439
  95.2 19.6 %all_to_all.19 = f32[64,1,128]{2,1,0:T(1,128)S(1)} all-to-all(f32[64,1,128]{2,1,0:T(1,128)S(1)} %get-tuple-element.131), channel_id=1, replica_groups=mesh['space'=16,'tracer'=4,'month'=4] {'space','tracer'}, dimensions={0} | all-to-all | bytes 65536 | tf_op jit(solution)/shard_map/all_to_all | solution.py:307
  114.8 0.1 reduce_sum.38
  114.9 8.0 %all_to_all.20.rows_ref = f32[4,1,128]{2,1,0:T(1,128)S(1)} all-to-all(f32[4,1,128]{2,1,0:T(1,128)S(1)} %broadcast_in_dim.10), channel_id=1, replica_groups=mesh['space'=16,'tracer'=4,'month'=4] {'month'}, dimensions={0} | all-to-all | bytes 4096 | tf_op jit(solution)/shard_map/all_to_all | solution.py:307
  122.8 1.3 %shard_map.111 = (f32[256,512]{1,0:T(8,128)S(1)}, f32[256,512]{1,0:T(8,128)}, f32[1,6]{1,0:T(1,128)S(1)}, f32[1,1]{1,0:T(1,128)}) custom-call(f32[4,1,128]{2,1,0:T(1,128)S(1)} %all_to_all.20.rows_ref, f32[256,512]{1,0:T(8,128)S(1)} %bitcast.15, f32[4,256,512]{2,1,0:T(8,128)S(1)} %bitcast.14), custom_call_target="tpu_custom_call" | custom-call | flops 2000000 | bytes 250000 | tf_op jit(solution)/shard_map/pallas_call | solution.py:451
  124.8 0.0 copy-start.5
  124.8 0.5 copy-done.5
  (43 shorter events, 0.2 us)
Async XLA Ops:
  0.6 7.4 %copy-start = (f32[4,8,4,8,512]{4,3,2,1,0:T(8,128)S(1)}, f32[4,8,4,8,512]{4,3,2,1,0:T(8,128)}, u32[]{:S(2)}) copy-start(f32[4,8,4,8,512]{4,3,2,1,0:T(8,128)} %refs_7_.1) | copy-start | bytes 6291460
  0.6 7.4 %copy-start.1 = (f32[8,4,8,512]{3,2,1,0:T(8,128)S(1)}, f32[8,4,8,512]{3,2,1,0:T(8,128)}, u32[]{:S(2)}) copy-start(f32[8,4,8,512]{3,2,1,0:T(8,128)} %refs_6_.1) | copy-start | bytes 1572868
  0.7 7.4 %copy-start.3 = (s32[8,512]{1,0:T(8,128)S(1)}, s32[8,512]{1,0:T(8,128)}, u32[]{:S(2)}) copy-start(s32[8,512]{1,0:T(8,128)} %depth_ref.1) | copy-start | bytes 49156
  0.7 7.4 %copy-start.2 = (s32[8,512]{1,0:T(8,128)S(1)}, s32[8,512]{1,0:T(8,128)}, u32[]{:S(2)}) copy-start(s32[8,512]{1,0:T(8,128)} %land_ref.1) | copy-start | bytes 49156
  0.7 7.4 %copy-start.4 = (f32[8]{0:T(128)S(1)}, f32[8]{0:T(128)}, u32[]{:S(2)}) copy-start(f32[8]{0:T(128)} %rates_ref.1) | copy-start | bytes 100
  2.2 9.7 %collective-permute-start.3 = (bf16[27,4,8,128]{3,2,1,0:T(8,128)(2,1)S(1)}, bf16[27,4,8,128]{3,2,1,0:T(8,128)(2,1)S(1)}, u32[]{:S(2)}, u32[]{:S(2)}) collective-permute-start(bf16[27,4,8,128]{3,2,1,0:T(8,128)(2,1)S(1)} %get-tuple-element.80), channel_id=1, source_target_pairs={{0,1},{1,2},{2,3},{3,0},{4,5},{5,6},{6,7},{7,4},{8,9},{9,10},{10,1... | collective-permute-start | bytes 663560 | tf_op jit(solution)/shard_map/ppermute | solution.py:316
  4.4 12.3 %collective-permute-start.4 = (bf16[27,4,8,128]{3,2,1,0:T(8,128)(2,1)S(1)}, bf16[27,4,8,128]{3,2,1,0:T(8,128)(2,1)S(1)}, u32[]{:S(2)}, u32[]{:S(2)}) collective-permute-start(bf16[27,4,8,128]{3,2,1,0:T(8,128)(2,1)S(1)} %get-tuple-element.81), channel_id=1, source_target_pairs={{0,2},{1,3},{2,0},{3,1},{4,6},{5,7},{6,4},{7,5},{8,10},{9,11},{10,... | collective-permute-start | bytes 663560 | tf_op jit(solution)/shard_map/ppermute | solution.py:316
  7.0 12.4 %collective-permute-start.5 = (bf16[27,4,8,128]{3,2,1,0:T(8,128)(2,1)S(1)}, bf16[27,4,8,128]{3,2,1,0:T(8,128)(2,1)S(1)}, u32[]{:S(2)}, u32[]{:S(2)}) collective-permute-start(bf16[27,4,8,128]{3,2,1,0:T(8,128)(2,1)S(1)} %get-tuple-element.82), channel_id=1, source_target_pairs={{0,3},{1,0},{2,1},{3,2},{4,7},{5,4},{6,5},{7,6},{8,11},{9,8},{10,9... | collective-permute-start | bytes 663560 | tf_op jit(solution)/shard_map/ppermute | solution.py:316
  8.9 10.8 %collective-permute-start.9 = (bf16[2,8,8,512]{3,2,1,0:T(8,128)(2,1)S(1)}, bf16[2,8,8,512]{3,2,1,0:T(8,128)(2,1)S(1)}, u32[]{:S(2)}, u32[]{:S(2)}) collective-permute-start(bf16[2,8,8,512]{3,2,1,0:T(8,128)(2,1)S(1)} %get-tuple-element.84), channel_id=1, source_target_pairs={{0,1},{1,2},{2,3},{3,0},{4,5},{5,6},{6,7},{7,4},{8,9},{9,10},{10,1... | collective-permute-start | bytes 393224 | tf_op jit(solution)/shard_map/ppermute | solution.py:316
  9.4 12.8 %collective-permute-start.2 = (bf16[27,4,8,128]{3,2,1,0:T(8,128)(2,1)S(1)}, bf16[27,4,8,128]{3,2,1,0:T(8,128)(2,1)S(1)}, u32[]{:S(2)}, u32[]{:S(2)}) collective-permute-start(bf16[27,4,8,128]{3,2,1,0:T(8,128)(2,1)S(1)} %get-tuple-element.106.refs_0_), channel_id=1, source_target_pairs={{0,12},{4,0},{8,4},{12,8},{1,13},{5,1},{9,5},{13,9},{2,14},{6,2},{... | collective-permute-start | bytes 663560 | tf_op jit(solution)/shard_map/ppermute | solution.py:316
  11.9 10.3 %collective-permute-start.10 = (bf16[2,8,8,512]{3,2,1,0:T(8,128)(2,1)S(1)}, bf16[2,8,8,512]{3,2,1,0:T(8,128)(2,1)S(1)}, u32[]{:S(2)}, u32[]{:S(2)}) collective-permute-start(bf16[2,8,8,512]{3,2,1,0:T(8,128)(2,1)S(1)} %get-tuple-element.85), channel_id=1, source_target_pairs={{0,3},{1,0},{2,1},{3,2},{4,7},{5,4},{6,5},{7,6},{8,11},{9,8},{10,9... | collective-permute-start | bytes 393224 | tf_op jit(solution)/shard_map/ppermute | solution.py:316
  16.6 6.3 %collective-permute-start.1 = (bf16[27,4,8,128]{3,2,1,0:T(8,128)(2,1)S(1)}, bf16[27,4,8,128]{3,2,1,0:T(8,128)(2,1)S(1)}, u32[]{:S(2)}, u32[]{:S(2)}) collective-permute-start(bf16[27,4,8,128]{3,2,1,0:T(8,128)(2,1)S(1)} %get-tuple-element.106.refs_0_), channel_id=1, source_target_pairs={{0,8},{4,12},{8,0},{12,4},{1,9},{5,13},{9,1},{13,5},{2,10},{6,14},... | collective-permute-start | bytes 663560 | tf_op jit(solution)/shard_map/ppermute | solution.py:316
  19.4 10.1 %collective-permute-start = (bf16[27,4,8,128]{3,2,1,0:T(8,128)(2,1)S(1)}, bf16[27,4,8,128]{3,2,1,0:T(8,128)(2,1)S(1)}, u32[]{:S(2)}, u32[]{:S(2)}) collective-permute-start(bf16[27,4,8,128]{3,2,1,0:T(8,128)(2,1)S(1)} %get-tuple-element.106.refs_0_), channel_id=1, source_target_pairs={{0,4},{4,8},{8,12},{12,0},{1,5},{5,9},{9,13},{13,1},{2,6},{6,10},{... | collective-permute-start | bytes 663560 | tf_op jit(solution)/shard_map/ppermute | solution.py:316
  19.7 12.7 %collective-permute-start.8 = (bf16[27,4,8,128]{3,2,1,0:T(8,128)(2,1)S(1)}, bf16[27,4,8,128]{3,2,1,0:T(8,128)(2,1)S(1)}, u32[]{:S(2)}, u32[]{:S(2)}) collective-permute-start(bf16[27,4,8,128]{3,2,1,0:T(8,128)(2,1)S(1)} %shard_map.86.refs_4_), channel_id=1, source_target_pairs={{0,12},{4,0},{8,4},{12,8},{1,13},{5,1},{9,5},{13,9},{2,14},{6,2},{... | collective-permute-start | bytes 663560 | tf_op jit(solution)/shard_map/ppermute | solution.py:316
  22.2 10.3 %collective-permute-start.7 = (bf16[27,4,8,128]{3,2,1,0:T(8,128)(2,1)S(1)}, bf16[27,4,8,128]{3,2,1,0:T(8,128)(2,1)S(1)}, u32[]{:S(2)}, u32[]{:S(2)}) collective-permute-start(bf16[27,4,8,128]{3,2,1,0:T(8,128)(2,1)S(1)} %shard_map.86.refs_4_), channel_id=1, source_target_pairs={{0,8},{4,12},{8,0},{12,4},{1,9},{5,13},{9,1},{13,5},{2,10},{6,14},... | collective-permute-start | bytes 663560 | tf_op jit(solution)/shard_map/ppermute | solution.py:316
  22.3 18.0 %collective-permute-start.6 = (bf16[27,4,8,128]{3,2,1,0:T(8,128)(2,1)S(1)}, bf16[27,4,8,128]{3,2,1,0:T(8,128)(2,1)S(1)}, u32[]{:S(2)}, u32[]{:S(2)}) collective-permute-start(bf16[27,4,8,128]{3,2,1,0:T(8,128)(2,1)S(1)} %shard_map.86.refs_4_), channel_id=1, source_target_pairs={{0,4},{4,8},{8,12},{12,0},{1,5},{5,9},{9,13},{13,1},{2,6},{6,10},{... | collective-permute-start | bytes 663560 | tf_op jit(solution)/shard_map/ppermute | solution.py:316
  22.9 30.4 %collective-permute-start.13 = (bf16[27,4,8,128]{3,2,1,0:T(8,128)(2,1)S(1)}, bf16[27,4,8,128]{3,2,1,0:T(8,128)(2,1)S(1)}, u32[]{:S(2)}, u32[]{:S(2)}) collective-permute-start(bf16[27,4,8,128]{3,2,1,0:T(8,128)(2,1)S(1)} %shard_map.89.refs_8_.refs_4_), channel_id=1, source_target_pairs={{0,12},{4,0},{8,4},{12,8},{1,13},{5,1},{9,5},{13,9},{2,14},{6,2},{... | collective-permute-start | bytes 663560 | tf_op jit(solution)/shard_map/ppermute | solution.py:316
  29.5 23.9 %collective-permute-start.12 = (bf16[27,4,8,128]{3,2,1,0:T(8,128)(2,1)S(1)}, bf16[27,4,8,128]{3,2,1,0:T(8,128)(2,1)S(1)}, u32[]{:S(2)}, u32[]{:S(2)}) collective-permute-start(bf16[27,4,8,128]{3,2,1,0:T(8,128)(2,1)S(1)} %shard_map.89.refs_8_.refs_4_), channel_id=1, source_target_pairs={{0,8},{4,12},{8,0},{12,4},{1,9},{5,13},{9,1},{13,5},{2,10},{6,14},... | collective-permute-start | bytes 663560 | tf_op jit(solution)/shard_map/ppermute | solution.py:316
  32.4 21.5 %collective-permute-start.11 = (bf16[27,4,8,128]{3,2,1,0:T(8,128)(2,1)S(1)}, bf16[27,4,8,128]{3,2,1,0:T(8,128)(2,1)S(1)}, u32[]{:S(2)}, u32[]{:S(2)}) collective-permute-start(bf16[27,4,8,128]{3,2,1,0:T(8,128)(2,1)S(1)} %shard_map.89.refs_8_.refs_4_), channel_id=1, source_target_pairs={{0,4},{4,8},{8,12},{12,0},{1,5},{5,9},{9,13},{13,1},{2,6},{6,10},{... | collective-permute-start | bytes 663560 | tf_op jit(solution)/shard_map/ppermute | solution.py:316
  32.4 17.7 %collective-permute-start.14 = (bf16[2,6,8,512]{3,2,1,0:T(8,128)(2,1)S(1)}, bf16[2,6,8,512]{3,2,1,0:T(8,128)(2,1)S(1)}, u32[]{:S(2)}, u32[]{:S(2)}) collective-permute-start(bf16[2,6,8,512]{3,2,1,0:T(8,128)(2,1)S(1)} %get-tuple-element.97), channel_id=1, source_target_pairs={{0,16},{16,32},{32,48},{48,64},{64,80},{80,96},{96,112},{112,128},... | collective-permute-start | bytes 294920 | tf_op jit(solution)/shard_map/ppermute | solution.py:316
  40.2 9.9 %collective-permute-start.15 = (bf16[2,6,8,512]{3,2,1,0:T(8,128)(2,1)S(1)}, bf16[2,6,8,512]{3,2,1,0:T(8,128)(2,1)S(1)}, u32[]{:S(2)}, u32[]{:S(2)}) collective-permute-start(bf16[2,6,8,512]{3,2,1,0:T(8,128)(2,1)S(1)} %get-tuple-element.98), channel_id=1, source_target_pairs={{0,240},{16,0},{32,16},{48,32},{64,48},{80,64},{96,80},{112,96},{1... | collective-permute-start | bytes 294920 | tf_op jit(solution)/shard_map/ppermute | solution.py:316
  50.5 6.7 %collective-permute-start.16 = (bf16[2,8,8,512]{3,2,1,0:T(8,128)(2,1)S(1)}, bf16[2,8,8,512]{3,2,1,0:T(8,128)(2,1)S(1)}, u32[]{:S(2)}, u32[]{:S(2)}) collective-permute-start(bf16[2,8,8,512]{3,2,1,0:T(8,128)(2,1)S(1)} %get-tuple-element.100), channel_id=1, source_target_pairs={{0,1},{1,2},{2,3},{3,0},{4,5},{5,6},{6,7},{7,4},{8,9},{9,10},{10,1... | collective-permute-start | bytes 393224 | tf_op jit(solution)/shard_map/ppermute | solution.py:316
  50.6 6.6 %collective-permute-start.17 = (bf16[2,8,8,512]{3,2,1,0:T(8,128)(2,1)S(1)}, bf16[2,8,8,512]{3,2,1,0:T(8,128)(2,1)S(1)}, u32[]{:S(2)}, u32[]{:S(2)}) collective-permute-start(bf16[2,8,8,512]{3,2,1,0:T(8,128)(2,1)S(1)} %get-tuple-element.101), channel_id=1, source_target_pairs={{0,3},{1,0},{2,1},{3,2},{4,7},{5,4},{6,5},{7,6},{8,11},{9,8},{10,9... | collective-permute-start | bytes 393224 | tf_op jit(solution)/shard_map/ppermute | solution.py:316
  53.3 6.6 %collective-permute-start.22 = (bf16[27,4,8,128]{3,2,1,0:T(8,128)(2,1)S(1)}, bf16[27,4,8,128]{3,2,1,0:T(8,128)(2,1)S(1)}, u32[]{:S(2)}, u32[]{:S(2)}) collective-permute-start(bf16[27,4,8,128]{3,2,1,0:T(8,128)(2,1)S(1)} %shard_map.98.refs_8_.refs_4_), channel_id=1, source_target_pairs={{0,12},{4,0},{8,4},{12,8},{1,13},{5,1},{9,5},{13,9},{2,14},{6,2},{... | collective-permute-start | bytes 663560 | tf_op jit(solution)/shard_map/ppermute | solution.py:316
  53.4 8.1 %collective-permute-start.21 = (bf16[27,4,8,128]{3,2,1,0:T(8,128)(2,1)S(1)}, bf16[27,4,8,128]{3,2,1,0:T(8,128)(2,1)S(1)}, u32[]{:S(2)}, u32[]{:S(2)}) collective-permute-start(bf16[27,4,8,128]{3,2,1,0:T(8,128)(2,1)S(1)} %shard_map.98.refs_8_.refs_4_), channel_id=1, source_target_pairs={{0,8},{4,12},{8,0},{12,4},{1,9},{5,13},{9,1},{13,5},{2,10},{6,14},... | collective-permute-start | bytes 663560 | tf_op jit(solution)/shard_map/ppermute | solution.py:316
  53.8 13.2 %collective-permute-start.20 = (bf16[27,4,8,128]{3,2,1,0:T(8,128)(2,1)S(1)}, bf16[27,4,8,128]{3,2,1,0:T(8,128)(2,1)S(1)}, u32[]{:S(2)}, u32[]{:S(2)}) collective-permute-start(bf16[27,4,8,128]{3,2,1,0:T(8,128)(2,1)S(1)} %shard_map.98.refs_8_.refs_4_), channel_id=1, source_target_pairs={{0,4},{4,8},{8,12},{12,0},{1,5},{5,9},{9,13},{13,1},{2,6},{6,10},{... | collective-permute-start | bytes 663560 | tf_op jit(solution)/shard_map/ppermute | solution.py:316
  57.2 12.1 %collective-permute-start.18 = (bf16[2,6,8,512]{3,2,1,0:T(8,128)(2,1)S(1)}, bf16[2,6,8,512]{3,2,1,0:T(8,128)(2,1)S(1)}, u32[]{:S(2)}, u32[]{:S(2)}) collective-permute-start(bf16[2,6,8,512]{3,2,1,0:T(8,128)(2,1)S(1)} %get-tuple-element.104), channel_id=1, source_target_pairs={{0,16},{16,32},{32,48},{48,64},{64,80},{80,96},{96,112},{112,128},... | collective-permute-start | bytes 294920 | tf_op jit(solution)/shard_map/ppermute | solution.py:316
  59.9 9.5 %collective-permute-start.19 = (bf16[2,6,8,512]{3,2,1,0:T(8,128)(2,1)S(1)}, bf16[2,6,8,512]{3,2,1,0:T(8,128)(2,1)S(1)}, u32[]{:S(2)}, u32[]{:S(2)}) collective-permute-start(bf16[2,6,8,512]{3,2,1,0:T(8,128)(2,1)S(1)} %get-tuple-element.105), channel_id=1, source_target_pairs={{0,240},{16,0},{32,16},{48,32},{64,48},{80,64},{96,80},{112,96},{1... | collective-permute-start | bytes 294920 | tf_op jit(solution)/shard_map/ppermute | solution.py:316
  69.7 5.9 %collective-permute-start.23 = (bf16[2,8,8,512]{3,2,1,0:T(8,128)(2,1)S(1)}, bf16[2,8,8,512]{3,2,1,0:T(8,128)(2,1)S(1)}, u32[]{:S(2)}, u32[]{:S(2)}) collective-permute-start(bf16[2,8,8,512]{3,2,1,0:T(8,128)(2,1)S(1)} %get-tuple-element.114), channel_id=1, source_target_pairs={{0,1},{1,2},{2,3},{3,0},{4,5},{5,6},{6,7},{7,4},{8,9},{9,10},{10,1... | collective-permute-start | bytes 393224 | tf_op jit(solution)/shard_map/ppermute | solution.py:316
  69.8 5.8 %collective-permute-start.24 = (bf16[2,8,8,512]{3,2,1,0:T(8,128)(2,1)S(1)}, bf16[2,8,8,512]{3,2,1,0:T(8,128)(2,1)S(1)}, u32[]{:S(2)}, u32[]{:S(2)}) collective-permute-start(bf16[2,8,8,512]{3,2,1,0:T(8,128)(2,1)S(1)} %get-tuple-element.115), channel_id=1, source_target_pairs={{0,3},{1,0},{2,1},{3,2},{4,7},{5,4},{6,5},{7,6},{8,11},{9,8},{10,9... | collective-permute-start | bytes 393224 | tf_op jit(solution)/shard_map/ppermute | solution.py:316
  75.6 5.2 %collective-permute-start.25 = (bf16[2,6,8,512]{3,2,1,0:T(8,128)(2,1)S(1)}, bf16[2,6,8,512]{3,2,1,0:T(8,128)(2,1)S(1)}, u32[]{:S(2)}, u32[]{:S(2)}) collective-permute-start(bf16[2,6,8,512]{3,2,1,0:T(8,128)(2,1)S(1)} %get-tuple-element.118), channel_id=1, source_target_pairs={{0,16},{16,32},{32,48},{48,64},{64,80},{80,96},{96,112},{112,128},... | collective-permute-start | bytes 294920 | tf_op jit(solution)/shard_map/ppermute | solution.py:316
  78.5 4.3 %collective-permute-start.26 = (bf16[2,6,8,512]{3,2,1,0:T(8,128)(2,1)S(1)}, bf16[2,6,8,512]{3,2,1,0:T(8,128)(2,1)S(1)}, u32[]{:S(2)}, u32[]{:S(2)}) collective-permute-start(bf16[2,6,8,512]{3,2,1,0:T(8,128)(2,1)S(1)} %get-tuple-element.119), channel_id=1, source_target_pairs={{0,240},{16,0},{32,16},{48,32},{64,48},{80,64},{96,80},{112,96},{1... | collective-permute-start | bytes 294920 | tf_op jit(solution)/shard_map/ppermute | solution.py:316
  83.1 5.1 %collective-permute-start.27 = (bf16[2,8,8,512]{3,2,1,0:T(8,128)(2,1)S(1)}, bf16[2,8,8,512]{3,2,1,0:T(8,128)(2,1)S(1)}, u32[]{:S(2)}, u32[]{:S(2)}) collective-permute-start(bf16[2,8,8,512]{3,2,1,0:T(8,128)(2,1)S(1)} %get-tuple-element.124), channel_id=1, source_target_pairs={{0,1},{1,2},{2,3},{3,0},{4,5},{5,6},{6,7},{7,4},{8,9},{9,10},{10,1... | collective-permute-start | bytes 393224 | tf_op jit(solution)/shard_map/ppermute | solution.py:316
  83.2 5.0 %collective-permute-start.28 = (bf16[2,8,8,512]{3,2,1,0:T(8,128)(2,1)S(1)}, bf16[2,8,8,512]{3,2,1,0:T(8,128)(2,1)S(1)}, u32[]{:S(2)}, u32[]{:S(2)}) collective-permute-start(bf16[2,8,8,512]{3,2,1,0:T(8,128)(2,1)S(1)} %get-tuple-element.125), channel_id=1, source_target_pairs={{0,3},{1,0},{2,1},{3,2},{4,7},{5,4},{6,5},{7,6},{8,11},{9,8},{10,9... | collective-permute-start | bytes 393224 | tf_op jit(solution)/shard_map/ppermute | solution.py:316
  88.2 3.9 %collective-permute-start.29 = (bf16[2,6,8,512]{3,2,1,0:T(8,128)(2,1)S(1)}, bf16[2,6,8,512]{3,2,1,0:T(8,128)(2,1)S(1)}, u32[]{:S(2)}, u32[]{:S(2)}) collective-permute-start(bf16[2,6,8,512]{3,2,1,0:T(8,128)(2,1)S(1)} %get-tuple-element.128), channel_id=1, source_target_pairs={{0,16},{16,32},{32,48},{48,64},{64,80},{80,96},{96,112},{112,128},... | collective-permute-start | bytes 294920 | tf_op jit(solution)/shard_map/ppermute | solution.py:316
  89.5 4.0 %collective-permute-start.30 = (bf16[2,6,8,512]{3,2,1,0:T(8,128)(2,1)S(1)}, bf16[2,6,8,512]{3,2,1,0:T(8,128)(2,1)S(1)}, u32[]{:S(2)}, u32[]{:S(2)}) collective-permute-start(bf16[2,6,8,512]{3,2,1,0:T(8,128)(2,1)S(1)} %get-tuple-element.129), channel_id=1, source_target_pairs={{0,240},{16,0},{32,16},{48,32},{64,48},{80,64},{96,80},{112,96},{1... | collective-permute-start | bytes 294920 | tf_op jit(solution)/shard_map/ppermute | solution.py:316
  124.8 0.5 copy-start.5
where the time goes:
time: 126 us; the launch traced here: 125 us
  starting transfers between devices  54 us (43%)
  blocking collectives  27.6 us (22%)
  Pallas kernels  22.9 us (18%)
  waiting for transfers between devices  18.6 us (15%)
  between operations  1.65 us (1%)
    ppermute x31, starting transfers between devices, shifted(): return lax.ppermute(x, axis, [(n, (n + by) % size) for n in range(size)])  54 us
    all_to_all x2, blocking collectives, spread(): return lax.all_to_all(x, axes, 0, 0, tiled=True)  27.6 us
    ppermute x31, waiting for transfers between devices, shifted(): return lax.ppermute(x, axis, [(n, (n + by) % size) for n in range(size)])  18.6 us
    pallas_call x8, Pallas kernels, part(): call(functools.partial(part_body, levels, columns, mine, is_outer), [(sha...  12.4 us
    pallas_call x4, Pallas kernels, prepared(): call(functools.partial(prepare_body, month, steps), [((27, levels, column...  3.23 us
  transfers between devices with their start and end apart: 31, of which 8 were waited for; matrix products, arithmetic and copies ran while one was open for 0% of the time, Pallas kernels for 14%

commit v1 on v0

--- a/solution.py
+++ b/solution.py
@@ -401,8 +401,12 @@
     turns = [fetched(after(of_turn(found, 0), gram))]
     found = lax.optimization_barrier((found, halos))[0]
     turns.append(fetched(of_turn(found, 1)))
+    turns += [fetched(of_turn(found, turn)) for turn in range(2, steps - 1)]
     for month in range(steps):
-        weights = prepared(own, turns, month) if month < 2 else next_weights
+        if month < 2:
+            weights = prepared(own, turns, month)
+        else:
+            weights = next_weights
         lev_lo, lev_hi, lon_lo, lon_hi = sent
         below, above = halos if month == 0 else (shifted(lev_hi, "month", 1), shifted(lev_lo, "month", -1))
         args = (weights, field_a, field_b, field_s, rate, wet)
@@ -422,10 +426,7 @@
             in_specs=[anywhere] + [vmem] * 4,
         )(new_a if month else wet, below, above, lon_lo, lon_hi)
         left, right = shifted(right, "space", 1), shifted(left, "space", -1)
-        if month == 0:
-            found = lax.optimization_barrier((found, left, right))[0]
-            turns += [fetched(of_turn(found, turn)) for turn in range(2, steps - 1)]
-        elif month < steps - 1:
+        if 0 < month < steps - 1:
             next_weights = prepared(own, turns, month + 1)
             left, right, next_weights = lax.optimization_barrier((left, right, next_weights))
         new_b = part(outer_levels, outer, True, below, above)

time: 126 us -> 126 us (level)
  no operation moved by 1% of the time
where the time goes in v1:
time: 126 us; the launch traced here: 125 us
  starting transfers between devices  54 us (43%)
  blocking collectives  27.6 us (22%)
  Pallas kernels  22.9 us (18%)
  waiting for transfers between devices  18.6 us (15%)
  between operations  1.65 us (1%)
    ppermute x31, starting transfers between devices, shifted(): return lax.ppermute(x, axis, [(n, (n + by) % size) for n in range(size)])  54 us
    all_to_all x2, blocking collectives, spread(): return lax.all_to_all(x, axes, 0, 0, tiled=True)  27.6 us
    ppermute x31, waiting for transfers between devices, shifted(): return lax.ppermute(x, axis, [(n, (n + by) % size) for n in range(size)])  18.6 us
    pallas_call x8, Pallas kernels, part(): call(functools.partial(part_body, levels, columns, mine, is_outer), [(sha...  12.4 us
    pallas_call x4, Pallas kernels, prepared(): call(functools.partial(prepare_body, month, steps), [((27, levels, column...  3.23 us
  transfers between devices with their start and end apart: 31, of which 8 were waited for; matrix products, arithmetic and copies ran while one was open for 0% of the time, Pallas kernels for 14%

profile of v1, /device:TPU:1, one launch (start us, length us, event | category | flops | bytes accessed | tf_op | source)
XLA Modules:
  0.0 125.3 jit_solution(15019518749445239499)
XLA Ops:
  0.7 1.5 %shard_map.85 = (bf16[27,4,8,128]{3,2,1,0:T(8,128)(2,1)S(1)}, bf16[27,4,8,128]{3,2,1,0:T(8,128)(2,1)S(1)}, bf16[27,4,8,128]{3,2,1,0:T(8,128)(2,1)S(1)}, bf16[27,4,8,128]{3,2,1,0:T(8,128)(2,1)S(1)}) custom-call(bf16[1,27,16,8,512]{4,3,2,1,0:T(8,128)(2,1)} %coef_ref.1), custom_call_target="tpu_custom_call" | custom-call | flops 1000000 | bytes 125000 | tf_op jit(solution)/shard_map/pallas_call | solution.py:339
  2.2 2.2 %collective-permute-start.3 = (bf16[27,4,8,128]{3,2,1,0:T(8,128)(2,1)S(1)}, bf16[27,4,8,128]{3,2,1,0:T(8,128)(2,1)S(1)}, u32[]{:S(2)}, u32[]{:S(2)}) collective-permute-start(bf16[27,4,8,128]{3,2,1,0:T(8,128)(2,1)S(1)} %get-tuple-element.76), channel_id=1, source_target_pairs={{0,1},{1,2},{2,3},{3,0},{4,5},{5,6},{6,7},{7,4},{8,9},{9,10},{10,1... | collective-permute-start | bytes 663560 | tf_op jit(solution)/shard_map/ppermute | solution.py:316
  4.4 2.6 %collective-permute-start.4 = (bf16[27,4,8,128]{3,2,1,0:T(8,128)(2,1)S(1)}, bf16[27,4,8,128]{3,2,1,0:T(8,128)(2,1)S(1)}, u32[]{:S(2)}, u32[]{:S(2)}) collective-permute-start(bf16[27,4,8,128]{3,2,1,0:T(8,128)(2,1)S(1)} %get-tuple-element.77), channel_id=1, source_target_pairs={{0,2},{1,3},{2,0},{3,1},{4,6},{5,7},{6,4},{7,5},{8,10},{9,11},{10,... | collective-permute-start | bytes 663560 | tf_op jit(solution)/shard_map/ppermute | solution.py:316
  7.0 1.1 collective-permute-start.5
  8.1 0.8 shard_map.88
  8.9 0.5 collective-permute-start.9
  9.4 2.5 %collective-permute-start.2 = (bf16[27,4,8,128]{3,2,1,0:T(8,128)(2,1)S(1)}, bf16[27,4,8,128]{3,2,1,0:T(8,128)(2,1)S(1)}, u32[]{:S(2)}, u32[]{:S(2)}) collective-permute-start(bf16[27,4,8,128]{3,2,1,0:T(8,128)(2,1)S(1)} %get-tuple-element.82.refs_0_), channel_id=1, source_target_pairs={{0,12},{4,0},{8,4},{12,8},{1,13},{5,1},{9,5},{13,9},{2,14},{6,2},{... | collective-permute-start | bytes 663560 | tf_op jit(solution)/shard_map/ppermute | solution.py:316
  11.9 2.3 %collective-permute-start.10 = (bf16[2,8,8,512]{3,2,1,0:T(8,128)(2,1)S(1)}, bf16[2,8,8,512]{3,2,1,0:T(8,128)(2,1)S(1)}, u32[]{:S(2)}, u32[]{:S(2)}) collective-permute-start(bf16[2,8,8,512]{3,2,1,0:T(8,128)(2,1)S(1)} %get-tuple-element.81), channel_id=1, source_target_pairs={{0,3},{1,0},{2,1},{3,2},{4,7},{5,4},{6,5},{7,6},{8,11},{9,8},{10,9... | collective-permute-start | bytes 393224 | tf_op jit(solution)/shard_map/ppermute | solution.py:316
  14.2 1.0 shard_map.87.refs_8_
  15.2 1.5 %collective-permute-done.4.refs_2_ = bf16[27,4,8,128]{3,2,1,0:T(8,128)(2,1)S(1)} collective-permute-done((bf16[27,4,8,128]{3,2,1,0:T(8,128)(2,1)S(1)}, bf16[27,4,8,128]{3,2,1,0:T(8,128)(2,1)S(1)}, u32[]{:S(2)}, u32[]{:S(2)}) %collective-permute-start.4) | collective-permute-done | bytes 221216 | tf_op jit(solution)/shard_map/ppermute | solution.py:316
  16.6 2.7 %collective-permute-start.1 = (bf16[27,4,8,128]{3,2,1,0:T(8,128)(2,1)S(1)}, bf16[27,4,8,128]{3,2,1,0:T(8,128)(2,1)S(1)}, u32[]{:S(2)}, u32[]{:S(2)}) collective-permute-start(bf16[27,4,8,128]{3,2,1,0:T(8,128)(2,1)S(1)} %get-tuple-element.82.refs_0_), channel_id=1, source_target_pairs={{0,8},{4,12},{8,0},{12,4},{1,9},{5,13},{9,1},{13,5},{2,10},{6,14},... | collective-permute-start | bytes 663560 | tf_op jit(solution)/shard_map/ppermute | solution.py:316
  19.4 0.0 collective-permute-done.5.refs_3_
  19.4 0.3 collective-permute-start
  19.7 2.4 %collective-permute-start.8 = (bf16[27,4,8,128]{3,2,1,0:T(8,128)(2,1)S(1)}, bf16[27,4,8,128]{3,2,1,0:T(8,128)(2,1)S(1)}, u32[]{:S(2)}, u32[]{:S(2)}) collective-permute-start(bf16[27,4,8,128]{3,2,1,0:T(8,128)(2,1)S(1)} %shard_map.86.refs_4_), channel_id=1, source_target_pairs={{0,12},{4,0},{8,4},{12,8},{1,13},{5,1},{9,5},{13,9},{2,14},{6,2},{... | collective-permute-start | bytes 663560 | tf_op jit(solution)/shard_map/ppermute | solution.py:316
  22.2 0.0 collective-permute-done.10.rest_1_.above_ref
  22.2 0.1 collective-permute-start.7
  22.3 0.6 collective-permute-start.6
  22.9 0.0 collective-permute-done.1.refs_2_
  22.9 2.5 %collective-permute-start.13 = (bf16[27,4,8,128]{3,2,1,0:T(8,128)(2,1)S(1)}, bf16[27,4,8,128]{3,2,1,0:T(8,128)(2,1)S(1)}, u32[]{:S(2)}, u32[]{:S(2)}) collective-permute-start(bf16[27,4,8,128]{3,2,1,0:T(8,128)(2,1)S(1)} %shard_map.89.refs_8_.refs_4_), channel_id=1, source_target_pairs={{0,12},{4,0},{8,4},{12,8},{1,13},{5,1},{9,5},{13,9},{2,14},{6,2},{... | collective-permute-start | bytes 663560 | tf_op jit(solution)/shard_map/ppermute | solution.py:316
  25.4 4.1 %collective-permute-done.refs_1_ = bf16[27,4,8,128]{3,2,1,0:T(8,128)(2,1)S(1)} collective-permute-done((bf16[27,4,8,128]{3,2,1,0:T(8,128)(2,1)S(1)}, bf16[27,4,8,128]{3,2,1,0:T(8,128)(2,1)S(1)}, u32[]{:S(2)}, u32[]{:S(2)}) %collective-permute-start) | collective-permute-done | bytes 221216 | tf_op jit(solution)/shard_map/ppermute | solution.py:316
  29.5 2.9 %collective-permute-start.12 = (bf16[27,4,8,128]{3,2,1,0:T(8,128)(2,1)S(1)}, bf16[27,4,8,128]{3,2,1,0:T(8,128)(2,1)S(1)}, u32[]{:S(2)}, u32[]{:S(2)}) collective-permute-start(bf16[27,4,8,128]{3,2,1,0:T(8,128)(2,1)S(1)} %shard_map.89.refs_8_.refs_4_), channel_id=1, source_target_pairs={{0,8},{4,12},{8,0},{12,4},{1,9},{5,13},{9,1},{13,5},{2,10},{6,14},... | collective-permute-start | bytes 663560 | tf_op jit(solution)/shard_map/ppermute | solution.py:316
  32.4 7.8 %collective-permute-start.14 = (bf16[2,6,8,512]{3,2,1,0:T(8,128)(2,1)S(1)}, bf16[2,6,8,512]{3,2,1,0:T(8,128)(2,1)S(1)}, u32[]{:S(2)}, u32[]{:S(2)}) collective-permute-start(bf16[2,6,8,512]{3,2,1,0:T(8,128)(2,1)S(1)} %get-tuple-element.93), channel_id=1, source_target_pairs={{0,16},{16,32},{32,48},{48,64},{64,80},{80,96},{96,112},{112,128},... | collective-permute-start | bytes 294920 | tf_op jit(solution)/shard_map/ppermute | solution.py:316
  40.2 5.7 %collective-permute-start.15 = (bf16[2,6,8,512]{3,2,1,0:T(8,128)(2,1)S(1)}, bf16[2,6,8,512]{3,2,1,0:T(8,128)(2,1)S(1)}, u32[]{:S(2)}, u32[]{:S(2)}) collective-permute-start(bf16[2,6,8,512]{3,2,1,0:T(8,128)(2,1)S(1)} %get-tuple-element.94), channel_id=1, source_target_pairs={{0,240},{16,0},{32,16},{48,32},{64,48},{80,64},{96,80},{112,96},{1... | collective-permute-start | bytes 294920 | tf_op jit(solution)/shard_map/ppermute | solution.py:316
  45.9 0.9 shard_map.91.wf_ref.refs_2_
  46.9 1.6 %shard_map.92.refs_0_.inner_ref = f32[2,2,8,8,512]{4,3,2,1,0:T(8,128)S(1)} custom-call(f32[27,4,8,512]{3,2,1,0:T(8,128)S(1)} %shard_map.91.wf_ref.refs_2_, f32[2,2,8,8,512]{4,3,2,1,0:T(8,128)S(1)} %get-tuple-element.86.inner_ref, f32[2,2,8,8,512]{4,3,2,1,0:T(8,128)S(1)} %get-tuple-element.87.outer_ref, f32[2,4,2,8,512]{4,3,2,1,0:T(8,128)S(1)} %get-tuple-element.88.sides_ref, ...), custom_call_target="tpu_custom_call" | custom-call | flops 10000000 | bytes 1250000 | tf_op jit(solution)/shard_map/pallas_call | solution.py:415
  48.5 1.6 %shard_map.93.refs_1_.outer_ref = f32[2,2,8,8,512]{4,3,2,1,0:T(8,128)S(1)} custom-call(f32[27,4,8,512]{3,2,1,0:T(8,128)S(1)} %shard_map.91.wf_ref.refs_2_, f32[2,2,8,8,512]{4,3,2,1,0:T(8,128)S(1)} %get-tuple-element.86.inner_ref, f32[2,2,8,8,512]{4,3,2,1,0:T(8,128)S(1)} %get-tuple-element.87.outer_ref, f32[2,4,2,8,512]{4,3,2,1,0:T(8,128)S(1)} %get-tuple-element.88.sides_ref, ...), custom_call_target="tpu_custom_call" | custom-call | flops 10000000 | bytes 1250000 | tf_op jit(solution)/shard_map/pallas_call | solution.py:415
  50.2 0.3 shard_map.95
  50.5 0.1 collective-permute-start.16
  50.6 2.7 %collective-permute-start.17 = (bf16[2,8,8,512]{3,2,1,0:T(8,128)(2,1)S(1)}, bf16[2,8,8,512]{3,2,1,0:T(8,128)(2,1)S(1)}, u32[]{:S(2)}, u32[]{:S(2)}) collective-permute-start(bf16[2,8,8,512]{3,2,1,0:T(8,128)(2,1)S(1)} %get-tuple-element.97), channel_id=1, source_target_pairs={{0,3},{1,0},{2,1},{3,2},{4,7},{5,4},{6,5},{7,6},{8,11},{9,8},{10,9... | collective-permute-start | bytes 393224 | tf_op jit(solution)/shard_map/ppermute | solution.py:316
  53.3 0.1 collective-permute-start.22
  53.4 0.5 collective-permute-start.21
  53.8 1.1 collective-permute-start.20
  54.9 0.8 shard_map.90.wf_ref.refs_2_
  55.7 1.5 %shard_map.96.after_ref.refs_0_.inner_ref = f32[2,2,8,8,512]{4,3,2,1,0:T(8,128)S(1)} custom-call(f32[27,4,8,512]{3,2,1,0:T(8,128)S(1)} %shard_map.90.wf_ref.refs_2_, f32[2,2,8,8,512]{4,3,2,1,0:T(8,128)S(1)} %shard_map.92.refs_0_.inner_ref, f32[2,2,8,8,512]{4,3,2,1,0:T(8,128)S(1)} %shard_map.93.refs_1_.outer_ref, ...), custom_call_target="tpu_custom_call" | custom-call | flops 10000000 | bytes 1250000 | tf_op jit(solution)/shard_map/pallas_call | solution.py:415
  57.2 2.7 %collective-permute-start.18 = (bf16[2,6,8,512]{3,2,1,0:T(8,128)(2,1)S(1)}, bf16[2,6,8,512]{3,2,1,0:T(8,128)(2,1)S(1)}, u32[]{:S(2)}, u32[]{:S(2)}) collective-permute-start(bf16[2,6,8,512]{3,2,1,0:T(8,128)(2,1)S(1)} %get-tuple-element.100), channel_id=1, source_target_pairs={{0,16},{16,32},{32,48},{48,64},{64,80},{80,96},{96,112},{112,128},... | collective-permute-start | bytes 294920 | tf_op jit(solution)/shard_map/ppermute | solution.py:316
  59.9 1.5 %collective-permute-done.21.refs_10_.refs_6_ = bf16[27,4,8,128]{3,2,1,0:T(8,128)(2,1)S(1)} collective-permute-done((bf16[27,4,8,128]{3,2,1,0:T(8,128)(2,1)S(1)}, bf16[27,4,8,128]{3,2,1,0:T(8,128)(2,1)S(1)}, u32[]{:S(2)}, u32[]{:S(2)}) %collective-permute-start.21) | collective-permute-done | bytes 221216 | tf_op jit(solution)/shard_map/ppermute | solution.py:316
  61.4 5.6 %collective-permute-done.20.refs_9_.refs_5_ = bf16[27,4,8,128]{3,2,1,0:T(8,128)(2,1)S(1)} collective-permute-done((bf16[27,4,8,128]{3,2,1,0:T(8,128)(2,1)S(1)}, bf16[27,4,8,128]{3,2,1,0:T(8,128)(2,1)S(1)}, u32[]{:S(2)}, u32[]{:S(2)}) %collective-permute-start.20) | collective-permute-done | bytes 221216 | tf_op jit(solution)/shard_map/ppermute | solution.py:316
  67.1 0.8 shard_map.99.wf_ref.refs_2_
  67.8 1.5 %shard_map.100.refs_1_.outer_ref = f32[2,2,8,8,512]{4,3,2,1,0:T(8,128)S(1)} custom-call(f32[27,4,8,512]{3,2,1,0:T(8,128)S(1)} %shard_map.90.wf_ref.refs_2_, f32[2,2,8,8,512]{4,3,2,1,0:T(8,128)S(1)} %shard_map.92.refs_0_.inner_ref, f32[2,2,8,8,512]{4,3,2,1,0:T(8,128)S(1)} %shard_map.93.refs_1_.outer_ref, ...), custom_call_target="tpu_custom_call" | custom-call | flops 10000000 | bytes 1250000 | tf_op jit(solution)/shard_map/pallas_call | solution.py:415
  69.4 0.3 shard_map.101
  69.7 0.1 collective-permute-start.23
  69.8 2.7 %collective-permute-start.24 = (bf16[2,8,8,512]{3,2,1,0:T(8,128)(2,1)S(1)}, bf16[2,8,8,512]{3,2,1,0:T(8,128)(2,1)S(1)}, u32[]{:S(2)}, u32[]{:S(2)}) collective-permute-start(bf16[2,8,8,512]{3,2,1,0:T(8,128)(2,1)S(1)} %get-tuple-element.107), channel_id=1, source_target_pairs={{0,3},{1,0},{2,1},{3,2},{4,7},{5,4},{6,5},{7,6},{8,11},{9,8},{10,9... | collective-permute-start | bytes 393224 | tf_op jit(solution)/shard_map/ppermute | solution.py:316
  72.5 1.5 %shard_map.102.after_ref.refs_0_.inner_ref = f32[2,2,8,8,512]{4,3,2,1,0:T(8,128)S(1)} custom-call(f32[27,4,8,512]{3,2,1,0:T(8,128)S(1)} %shard_map.99.wf_ref.refs_2_, f32[2,2,8,8,512]{4,3,2,1,0:T(8,128)S(1)} %shard_map.96.after_ref.refs_0_.inner_ref, f32[2,2,8,8,512]{4,3,2,1,0:T(8,128)S(1)} %shard_map.100.refs_1_.outer_ref, ...), custom_call_target="tpu_custom_call" | custom-call | flops 10000000 | bytes 1250000 | tf_op jit(solution)/shard_map/pallas_call | solution.py:415
  74.0 1.6 %collective-permute-done.23.below_ref.rest_0_ = bf16[2,8,8,512]{3,2,1,0:T(8,128)(2,1)S(1)} collective-permute-done((bf16[2,8,8,512]{3,2,1,0:T(8,128)(2,1)S(1)}, bf16[2,8,8,512]{3,2,1,0:T(8,128)(2,1)S(1)}, u32[]{:S(2)}, u32[]{:S(2)}) %collective-permute-start.23) | collective-permute-done | bytes 131104 | tf_op jit(solution)/shard_map/ppermute | solution.py:316
  75.6 2.9 %collective-permute-start.25 = (bf16[2,6,8,512]{3,2,1,0:T(8,128)(2,1)S(1)}, bf16[2,6,8,512]{3,2,1,0:T(8,128)(2,1)S(1)}, u32[]{:S(2)}, u32[]{:S(2)}) collective-permute-start(bf16[2,6,8,512]{3,2,1,0:T(8,128)(2,1)S(1)} %get-tuple-element.110), channel_id=1, source_target_pairs={{0,16},{16,32},{32,48},{48,64},{64,80},{80,96},{96,112},{112,128},... | collective-permute-start | bytes 294920 | tf_op jit(solution)/shard_map/ppermute | solution.py:316
  78.5 0.8 shard_map.104.wf_ref.refs_2_
  79.2 1.5 %shard_map.105.refs_1_.outer_ref = f32[2,2,8,8,512]{4,3,2,1,0:T(8,128)S(1)} custom-call(f32[27,4,8,512]{3,2,1,0:T(8,128)S(1)} %shard_map.99.wf_ref.refs_2_, f32[2,2,8,8,512]{4,3,2,1,0:T(8,128)S(1)} %shard_map.96.after_ref.refs_0_.inner_ref, f32[2,2,8,8,512]{4,3,2,1,0:T(8,128)S(1)} %shard_map.100.refs_1_.outer_ref, ...), custom_call_target="tpu_custom_call" | custom-call | flops 10000000 | bytes 1250000 | tf_op jit(solution)/shard_map/pallas_call | solution.py:415
  80.8 2.0 %collective-permute-done.26.refs_4_ = bf16[2,6,8,512]{3,2,1,0:T(8,128)(2,1)S(1)} collective-permute-done((bf16[2,6,8,512]{3,2,1,0:T(8,128)(2,1)S(1)}, bf16[2,6,8,512]{3,2,1,0:T(8,128)(2,1)S(1)}, u32[]{:S(2)}, u32[]{:S(2)}) %collective-permute-start.26) | collective-permute-done | bytes 98336 | tf_op jit(solution)/shard_map/ppermute | solution.py:316
  82.8 0.3 shard_map.106
  83.1 0.1 collective-permute-start.27
  83.2 2.8 %collective-permute-start.28 = (bf16[2,8,8,512]{3,2,1,0:T(8,128)(2,1)S(1)}, bf16[2,8,8,512]{3,2,1,0:T(8,128)(2,1)S(1)}, u32[]{:S(2)}, u32[]{:S(2)}) collective-permute-start(bf16[2,8,8,512]{3,2,1,0:T(8,128)(2,1)S(1)} %get-tuple-element.117), channel_id=1, source_target_pairs={{0,3},{1,0},{2,1},{3,2},{4,7},{5,4},{6,5},{7,6},{8,11},{9,8},{10,9... | collective-permute-start | bytes 393224 | tf_op jit(solution)/shard_map/ppermute | solution.py:316
  85.9 1.5 %shard_map.107.after_ref.refs_0_ = f32[2,2,8,8,512]{4,3,2,1,0:T(8,128)S(1)} custom-call(f32[27,4,8,512]{3,2,1,0:T(8,128)S(1)} %shard_map.104.wf_ref.refs_2_, f32[2,2,8,8,512]{4,3,2,1,0:T(8,128)S(1)} %shard_map.102.after_ref.refs_0_.inner_ref, f32[2,2,8,8,512]{4,3,2,1,0:T(8,128)S(1)} %shard_map.105.refs_1_.outer_ref, ...), custom_call_target="tpu_custom_call" | custom-call | flops 10000000 | bytes 1250000 | tf_op jit(solution)/shard_map/pallas_call | solution.py:415
  87.5 0.7 collective-permute-done.27.rest_0_.below_ref
  88.2 1.3 %collective-permute-start.29 = (bf16[2,6,8,512]{3,2,1,0:T(8,128)(2,1)S(1)}, bf16[2,6,8,512]{3,2,1,0:T(8,128)(2,1)S(1)}, u32[]{:S(2)}, u32[]{:S(2)}) collective-permute-start(bf16[2,6,8,512]{3,2,1,0:T(8,128)(2,1)S(1)} %get-tuple-element.120), channel_id=1, source_target_pairs={{0,16},{16,32},{32,48},{48,64},{64,80},{80,96},{96,112},{112,128},... | collective-permute-start | bytes 294920 | tf_op jit(solution)/shard_map/ppermute | solution.py:316
  89.5 1.0 collective-permute-start.30
  90.5 1.6 %shard_map.108.refs_1_ = f32[2,2,8,8,512]{4,3,2,1,0:T(8,128)S(1)} custom-call(f32[27,4,8,512]{3,2,1,0:T(8,128)S(1)} %shard_map.104.wf_ref.refs_2_, f32[2,2,8,8,512]{4,3,2,1,0:T(8,128)S(1)} %shard_map.102.after_ref.refs_0_.inner_ref, f32[2,2,8,8,512]{4,3,2,1,0:T(8,128)S(1)} %shard_map.105.refs_1_.outer_ref, ...), custom_call_target="tpu_custom_call" | custom-call | flops 10000000 | bytes 1250000 | tf_op jit(solution)/shard_map/pallas_call | solution.py:415
  92.1 1.5 %collective-permute-done.30.refs_4_ = bf16[2,6,8,512]{3,2,1,0:T(8,128)(2,1)S(1)} collective-permute-done((bf16[2,6,8,512]{3,2,1,0:T(8,128)(2,1)S(1)}, bf16[2,6,8,512]{3,2,1,0:T(8,128)(2,1)S(1)}, u32[]{:S(2)}, u32[]{:S(2)}) %collective-permute-start.30) | collective-permute-done | bytes 98336 | tf_op jit(solution)/shard_map/ppermute | solution.py:316
  93.6 1.6 %shard_map.110 = (f32[8,4,8,512]{3,2,1,0:T(8,128)}, f32[8,4,8,512]{3,2,1,0:T(8,128)S(1)}, f32[64,1,128]{2,1,0:T(1,128)S(1)}) custom-call(f32[2,2,8,8,512]{4,3,2,1,0:T(8,128)S(1)} %shard_map.107.after_ref.refs_0_, f32[2,2,8,8,512]{4,3,2,1,0:T(8,128)S(1)} %shard_map.108.refs_1_, f32[27,4,8,512]{3,2,1,0:T(8,128)S(1)} %shard_map.104.wf_ref.refs_2_, ...), custom_call_target="tpu_custom_call" | custom-call | flops 4000000 | bytes 500000 | tf_op jit(solution)/shard_map/pallas_call | solution.py:440
  95.2 19.6 %all_to_all.19 = f32[64,1,128]{2,1,0:T(1,128)S(1)} all-to-all(f32[64,1,128]{2,1,0:T(1,128)S(1)} %get-tuple-element.123), channel_id=1, replica_groups=mesh['space'=16,'tracer'=4,'month'=4] {'space','tracer'}, dimensions={0} | all-to-all | bytes 65536 | tf_op jit(solution)/shard_map/all_to_all | solution.py:307
  114.8 0.1 reduce_sum.38
  114.9 8.0 %all_to_all.20.rows_ref = f32[4,1,128]{2,1,0:T(1,128)S(1)} all-to-all(f32[4,1,128]{2,1,0:T(1,128)S(1)} %broadcast_in_dim.10), channel_id=1, replica_groups=mesh['space'=16,'tracer'=4,'month'=4] {'month'}, dimensions={0} | all-to-all | bytes 4096 | tf_op jit(solution)/shard_map/all_to_all | solution.py:307
  122.8 1.3 %shard_map.111 = (f32[256,512]{1,0:T(8,128)S(1)}, f32[256,512]{1,0:T(8,128)}, f32[1,6]{1,0:T(1,128)S(1)}, f32[1,1]{1,0:T(1,128)}) custom-call(f32[4,1,128]{2,1,0:T(1,128)S(1)} %all_to_all.20.rows_ref, f32[256,512]{1,0:T(8,128)S(1)} %bitcast.15, f32[4,256,512]{2,1,0:T(8,128)S(1)} %bitcast.14), custom_call_target="tpu_custom_call" | custom-call | flops 2000000 | bytes 250000 | tf_op jit(solution)/shard_map/pallas_call | solution.py:452
  124.8 0.0 copy-start.5
  124.8 0.5 copy-done.5
  (43 shorter events, 0.2 us)
Async XLA Ops:
  0.6 7.4 %copy-start = (f32[4,8,4,8,512]{4,3,2,1,0:T(8,128)S(1)}, f32[4,8,4,8,512]{4,3,2,1,0:T(8,128)}, u32[]{:S(2)}) copy-start(f32[4,8,4,8,512]{4,3,2,1,0:T(8,128)} %refs_7_.1) | copy-start | bytes 6291460
  0.6 7.4 %copy-start.1 = (f32[8,4,8,512]{3,2,1,0:T(8,128)S(1)}, f32[8,4,8,512]{3,2,1,0:T(8,128)}, u32[]{:S(2)}) copy-start(f32[8,4,8,512]{3,2,1,0:T(8,128)} %refs_6_.1) | copy-start | bytes 1572868
  0.7 7.4 %copy-start.3 = (s32[8,512]{1,0:T(8,128)S(1)}, s32[8,512]{1,0:T(8,128)}, u32[]{:S(2)}) copy-start(s32[8,512]{1,0:T(8,128)} %depth_ref.1) | copy-start | bytes 49156
  0.7 7.4 %copy-start.2 = (s32[8,512]{1,0:T(8,128)S(1)}, s32[8,512]{1,0:T(8,128)}, u32[]{:S(2)}) copy-start(s32[8,512]{1,0:T(8,128)} %land_ref.1) | copy-start | bytes 49156
  0.7 7.4 %copy-start.4 = (f32[8]{0:T(128)S(1)}, f32[8]{0:T(128)}, u32[]{:S(2)}) copy-start(f32[8]{0:T(128)} %rates_ref.1) | copy-start | bytes 100
  2.2 9.7 %collective-permute-start.3 = (bf16[27,4,8,128]{3,2,1,0:T(8,128)(2,1)S(1)}, bf16[27,4,8,128]{3,2,1,0:T(8,128)(2,1)S(1)}, u32[]{:S(2)}, u32[]{:S(2)}) collective-permute-start(bf16[27,4,8,128]{3,2,1,0:T(8,128)(2,1)S(1)} %get-tuple-element.76), channel_id=1, source_target_pairs={{0,1},{1,2},{2,3},{3,0},{4,5},{5,6},{6,7},{7,4},{8,9},{9,10},{10,1... | collective-permute-start | bytes 663560 | tf_op jit(solution)/shard_map/ppermute | solution.py:316
  4.4 12.3 %collective-permute-start.4 = (bf16[27,4,8,128]{3,2,1,0:T(8,128)(2,1)S(1)}, bf16[27,4,8,128]{3,2,1,0:T(8,128)(2,1)S(1)}, u32[]{:S(2)}, u32[]{:S(2)}) collective-permute-start(bf16[27,4,8,128]{3,2,1,0:T(8,128)(2,1)S(1)} %get-tuple-element.77), channel_id=1, source_target_pairs={{0,2},{1,3},{2,0},{3,1},{4,6},{5,7},{6,4},{7,5},{8,10},{9,11},{10,... | collective-permute-start | bytes 663560 | tf_op jit(solution)/shard_map/ppermute | solution.py:316
  7.0 12.4 %collective-permute-start.5 = (bf16[27,4,8,128]{3,2,1,0:T(8,128)(2,1)S(1)}, bf16[27,4,8,128]{3,2,1,0:T(8,128)(2,1)S(1)}, u32[]{:S(2)}, u32[]{:S(2)}) collective-permute-start(bf16[27,4,8,128]{3,2,1,0:T(8,128)(2,1)S(1)} %get-tuple-element.78), channel_id=1, source_target_pairs={{0,3},{1,0},{2,1},{3,2},{4,7},{5,4},{6,5},{7,6},{8,11},{9,8},{10,9... | collective-permute-start | bytes 663560 | tf_op jit(solution)/shard_map/ppermute | solution.py:316
  8.9 10.8 %collective-permute-start.9 = (bf16[2,8,8,512]{3,2,1,0:T(8,128)(2,1)S(1)}, bf16[2,8,8,512]{3,2,1,0:T(8,128)(2,1)S(1)}, u32[]{:S(2)}, u32[]{:S(2)}) collective-permute-start(bf16[2,8,8,512]{3,2,1,0:T(8,128)(2,1)S(1)} %get-tuple-element.80), channel_id=1, source_target_pairs={{0,1},{1,2},{2,3},{3,0},{4,5},{5,6},{6,7},{7,4},{8,9},{9,10},{10,1... | collective-permute-start | bytes 393224 | tf_op jit(solution)/shard_map/ppermute | solution.py:316
  9.4 12.8 %collective-permute-start.2 = (bf16[27,4,8,128]{3,2,1,0:T(8,128)(2,1)S(1)}, bf16[27,4,8,128]{3,2,1,0:T(8,128)(2,1)S(1)}, u32[]{:S(2)}, u32[]{:S(2)}) collective-permute-start(bf16[27,4,8,128]{3,2,1,0:T(8,128)(2,1)S(1)} %get-tuple-element.82.refs_0_), channel_id=1, source_target_pairs={{0,12},{4,0},{8,4},{12,8},{1,13},{5,1},{9,5},{13,9},{2,14},{6,2},{... | collective-permute-start | bytes 663560 | tf_op jit(solution)/shard_map/ppermute | solution.py:316
  11.9 10.3 %collective-permute-start.10 = (bf16[2,8,8,512]{3,2,1,0:T(8,128)(2,1)S(1)}, bf16[2,8,8,512]{3,2,1,0:T(8,128)(2,1)S(1)}, u32[]{:S(2)}, u32[]{:S(2)}) collective-permute-start(bf16[2,8,8,512]{3,2,1,0:T(8,128)(2,1)S(1)} %get-tuple-element.81), channel_id=1, source_target_pairs={{0,3},{1,0},{2,1},{3,2},{4,7},{5,4},{6,5},{7,6},{8,11},{9,8},{10,9... | collective-permute-start | bytes 393224 | tf_op jit(solution)/shard_map/ppermute | solution.py:316
  16.6 6.3 %collective-permute-start.1 = (bf16[27,4,8,128]{3,2,1,0:T(8,128)(2,1)S(1)}, bf16[27,4,8,128]{3,2,1,0:T(8,128)(2,1)S(1)}, u32[]{:S(2)}, u32[]{:S(2)}) collective-permute-start(bf16[27,4,8,128]{3,2,1,0:T(8,128)(2,1)S(1)} %get-tuple-element.82.refs_0_), channel_id=1, source_target_pairs={{0,8},{4,12},{8,0},{12,4},{1,9},{5,13},{9,1},{13,5},{2,10},{6,14},... | collective-permute-start | bytes 663560 | tf_op jit(solution)/shard_map/ppermute | solution.py:316
  19.4 10.1 %collective-permute-start = (bf16[27,4,8,128]{3,2,1,0:T(8,128)(2,1)S(1)}, bf16[27,4,8,128]{3,2,1,0:T(8,128)(2,1)S(1)}, u32[]{:S(2)}, u32[]{:S(2)}) collective-permute-start(bf16[27,4,8,128]{3,2,1,0:T(8,128)(2,1)S(1)} %get-tuple-element.82.refs_0_), channel_id=1, source_target_pairs={{0,4},{4,8},{8,12},{12,0},{1,5},{5,9},{9,13},{13,1},{2,6},{6,10},{... | collective-permute-start | bytes 663560 | tf_op jit(solution)/shard_map/ppermute | solution.py:316
  19.7 12.7 %collective-permute-start.8 = (bf16[27,4,8,128]{3,2,1,0:T(8,128)(2,1)S(1)}, bf16[27,4,8,128]{3,2,1,0:T(8,128)(2,1)S(1)}, u32[]{:S(2)}, u32[]{:S(2)}) collective-permute-start(bf16[27,4,8,128]{3,2,1,0:T(8,128)(2,1)S(1)} %shard_map.86.refs_4_), channel_id=1, source_target_pairs={{0,12},{4,0},{8,4},{12,8},{1,13},{5,1},{9,5},{13,9},{2,14},{6,2},{... | collective-permute-start | bytes 663560 | tf_op jit(solution)/shard_map/ppermute | solution.py:316
  22.2 10.3 %collective-permute-start.7 = (bf16[27,4,8,128]{3,2,1,0:T(8,128)(2,1)S(1)}, bf16[27,4,8,128]{3,2,1,0:T(8,128)(2,1)S(1)}, u32[]{:S(2)}, u32[]{:S(2)}) collective-permute-start(bf16[27,4,8,128]{3,2,1,0:T(8,128)(2,1)S(1)} %shard_map.86.refs_4_), channel_id=1, source_target_pairs={{0,8},{4,12},{8,0},{12,4},{1,9},{5,13},{9,1},{13,5},{2,10},{6,14},... | collective-permute-start | bytes 663560 | tf_op jit(solution)/shard_map/ppermute | solution.py:316
  22.3 18.0 %collective-permute-start.6 = (bf16[27,4,8,128]{3,2,1,0:T(8,128)(2,1)S(1)}, bf16[27,4,8,128]{3,2,1,0:T(8,128)(2,1)S(1)}, u32[]{:S(2)}, u32[]{:S(2)}) collective-permute-start(bf16[27,4,8,128]{3,2,1,0:T(8,128)(2,1)S(1)} %shard_map.86.refs_4_), channel_id=1, source_target_pairs={{0,4},{4,8},{8,12},{12,0},{1,5},{5,9},{9,13},{13,1},{2,6},{6,10},{... | collective-permute-start | bytes 663560 | tf_op jit(solution)/shard_map/ppermute | solution.py:316
  22.9 30.4 %collective-permute-start.13 = (bf16[27,4,8,128]{3,2,1,0:T(8,128)(2,1)S(1)}, bf16[27,4,8,128]{3,2,1,0:T(8,128)(2,1)S(1)}, u32[]{:S(2)}, u32[]{:S(2)}) collective-permute-start(bf16[27,4,8,128]{3,2,1,0:T(8,128)(2,1)S(1)} %shard_map.89.refs_8_.refs_4_), channel_id=1, source_target_pairs={{0,12},{4,0},{8,4},{12,8},{1,13},{5,1},{9,5},{13,9},{2,14},{6,2},{... | collective-permute-start | bytes 663560 | tf_op jit(solution)/shard_map/ppermute | solution.py:316
  29.5 23.9 %collective-permute-start.12 = (bf16[27,4,8,128]{3,2,1,0:T(8,128)(2,1)S(1)}, bf16[27,4,8,128]{3,2,1,0:T(8,128)(2,1)S(1)}, u32[]{:S(2)}, u32[]{:S(2)}) collective-permute-start(bf16[27,4,8,128]{3,2,1,0:T(8,128)(2,1)S(1)} %shard_map.89.refs_8_.refs_4_), channel_id=1, source_target_pairs={{0,8},{4,12},{8,0},{12,4},{1,9},{5,13},{9,1},{13,5},{2,10},{6,14},... | collective-permute-start | bytes 663560 | tf_op jit(solution)/shard_map/ppermute | solution.py:316
  32.4 21.5 %collective-permute-start.11 = (bf16[27,4,8,128]{3,2,1,0:T(8,128)(2,1)S(1)}, bf16[27,4,8,128]{3,2,1,0:T(8,128)(2,1)S(1)}, u32[]{:S(2)}, u32[]{:S(2)}) collective-permute-start(bf16[27,4,8,128]{3,2,1,0:T(8,128)(2,1)S(1)} %shard_map.89.refs_8_.refs_4_), channel_id=1, source_target_pairs={{0,4},{4,8},{8,12},{12,0},{1,5},{5,9},{9,13},{13,1},{2,6},{6,10},{... | collective-permute-start | bytes 663560 | tf_op jit(solution)/shard_map/ppermute | solution.py:316
  32.4 17.7 %collective-permute-start.14 = (bf16[2,6,8,512]{3,2,1,0:T(8,128)(2,1)S(1)}, bf16[2,6,8,512]{3,2,1,0:T(8,128)(2,1)S(1)}, u32[]{:S(2)}, u32[]{:S(2)}) collective-permute-start(bf16[2,6,8,512]{3,2,1,0:T(8,128)(2,1)S(1)} %get-tuple-element.93), channel_id=1, source_target_pairs={{0,16},{16,32},{32,48},{48,64},{64,80},{80,96},{96,112},{112,128},... | collective-permute-start | bytes 294920 | tf_op jit(solution)/shard_map/ppermute | solution.py:316
  40.2 9.9 %collective-permute-start.15 = (bf16[2,6,8,512]{3,2,1,0:T(8,128)(2,1)S(1)}, bf16[2,6,8,512]{3,2,1,0:T(8,128)(2,1)S(1)}, u32[]{:S(2)}, u32[]{:S(2)}) collective-permute-start(bf16[2,6,8,512]{3,2,1,0:T(8,128)(2,1)S(1)} %get-tuple-element.94), channel_id=1, source_target_pairs={{0,240},{16,0},{32,16},{48,32},{64,48},{80,64},{96,80},{112,96},{1... | collective-permute-start | bytes 294920 | tf_op jit(solution)/shard_map/ppermute | solution.py:316
  50.5 6.7 %collective-permute-start.16 = (bf16[2,8,8,512]{3,2,1,0:T(8,128)(2,1)S(1)}, bf16[2,8,8,512]{3,2,1,0:T(8,128)(2,1)S(1)}, u32[]{:S(2)}, u32[]{:S(2)}) collective-permute-start(bf16[2,8,8,512]{3,2,1,0:T(8,128)(2,1)S(1)} %get-tuple-element.96), channel_id=1, source_target_pairs={{0,1},{1,2},{2,3},{3,0},{4,5},{5,6},{6,7},{7,4},{8,9},{9,10},{10,1... | collective-permute-start | bytes 393224 | tf_op jit(solution)/shard_map/ppermute | solution.py:316
  50.6 6.6 %collective-permute-start.17 = (bf16[2,8,8,512]{3,2,1,0:T(8,128)(2,1)S(1)}, bf16[2,8,8,512]{3,2,1,0:T(8,128)(2,1)S(1)}, u32[]{:S(2)}, u32[]{:S(2)}) collective-permute-start(bf16[2,8,8,512]{3,2,1,0:T(8,128)(2,1)S(1)} %get-tuple-element.97), channel_id=1, source_target_pairs={{0,3},{1,0},{2,1},{3,2},{4,7},{5,4},{6,5},{7,6},{8,11},{9,8},{10,9... | collective-permute-start | bytes 393224 | tf_op jit(solution)/shard_map/ppermute | solution.py:316
  53.3 6.6 %collective-permute-start.22 = (bf16[27,4,8,128]{3,2,1,0:T(8,128)(2,1)S(1)}, bf16[27,4,8,128]{3,2,1,0:T(8,128)(2,1)S(1)}, u32[]{:S(2)}, u32[]{:S(2)}) collective-permute-start(bf16[27,4,8,128]{3,2,1,0:T(8,128)(2,1)S(1)} %shard_map.98.refs_8_.refs_4_), channel_id=1, source_target_pairs={{0,12},{4,0},{8,4},{12,8},{1,13},{5,1},{9,5},{13,9},{2,14},{6,2},{... | collective-permute-start | bytes 663560 | tf_op jit(solution)/shard_map/ppermute | solution.py:316
  53.4 8.1 %collective-permute-start.21 = (bf16[27,4,8,128]{3,2,1,0:T(8,128)(2,1)S(1)}, bf16[27,4,8,128]{3,2,1,0:T(8,128)(2,1)S(1)}, u32[]{:S(2)}, u32[]{:S(2)}) collective-permute-start(bf16[27,4,8,128]{3,2,1,0:T(8,128)(2,1)S(1)} %shard_map.98.refs_8_.refs_4_), channel_id=1, source_target_pairs={{0,8},{4,12},{8,0},{12,4},{1,9},{5,13},{9,1},{13,5},{2,10},{6,14},... | collective-permute-start | bytes 663560 | tf_op jit(solution)/shard_map/ppermute | solution.py:316
  53.8 13.2 %collective-permute-start.20 = (bf16[27,4,8,128]{3,2,1,0:T(8,128)(2,1)S(1)}, bf16[27,4,8,128]{3,2,1,0:T(8,128)(2,1)S(1)}, u32[]{:S(2)}, u32[]{:S(2)}) collective-permute-start(bf16[27,4,8,128]{3,2,1,0:T(8,128)(2,1)S(1)} %shard_map.98.refs_8_.refs_4_), channel_id=1, source_target_pairs={{0,4},{4,8},{8,12},{12,0},{1,5},{5,9},{9,13},{13,1},{2,6},{6,10},{... | collective-permute-start | bytes 663560 | tf_op jit(solution)/shard_map/ppermute | solution.py:316
  57.2 12.1 %collective-permute-start.18 = (bf16[2,6,8,512]{3,2,1,0:T(8,128)(2,1)S(1)}, bf16[2,6,8,512]{3,2,1,0:T(8,128)(2,1)S(1)}, u32[]{:S(2)}, u32[]{:S(2)}) collective-permute-start(bf16[2,6,8,512]{3,2,1,0:T(8,128)(2,1)S(1)} %get-tuple-element.100), channel_id=1, source_target_pairs={{0,16},{16,32},{32,48},{48,64},{64,80},{80,96},{96,112},{112,128},... | collective-permute-start | bytes 294920 | tf_op jit(solution)/shard_map/ppermute | solution.py:316
  59.9 9.5 %collective-permute-start.19 = (bf16[2,6,8,512]{3,2,1,0:T(8,128)(2,1)S(1)}, bf16[2,6,8,512]{3,2,1,0:T(8,128)(2,1)S(1)}, u32[]{:S(2)}, u32[]{:S(2)}) collective-permute-start(bf16[2,6,8,512]{3,2,1,0:T(8,128)(2,1)S(1)} %get-tuple-element.101), channel_id=1, source_target_pairs={{0,240},{16,0},{32,16},{48,32},{64,48},{80,64},{96,80},{112,96},{1... | collective-permute-start | bytes 294920 | tf_op jit(solution)/shard_map/ppermute | solution.py:316
  69.7 5.9 %collective-permute-start.23 = (bf16[2,8,8,512]{3,2,1,0:T(8,128)(2,1)S(1)}, bf16[2,8,8,512]{3,2,1,0:T(8,128)(2,1)S(1)}, u32[]{:S(2)}, u32[]{:S(2)}) collective-permute-start(bf16[2,8,8,512]{3,2,1,0:T(8,128)(2,1)S(1)} %get-tuple-element.106), channel_id=1, source_target_pairs={{0,1},{1,2},{2,3},{3,0},{4,5},{5,6},{6,7},{7,4},{8,9},{9,10},{10,1... | collective-permute-start | bytes 393224 | tf_op jit(solution)/shard_map/ppermute | solution.py:316
  69.8 5.8 %collective-permute-start.24 = (bf16[2,8,8,512]{3,2,1,0:T(8,128)(2,1)S(1)}, bf16[2,8,8,512]{3,2,1,0:T(8,128)(2,1)S(1)}, u32[]{:S(2)}, u32[]{:S(2)}) collective-permute-start(bf16[2,8,8,512]{3,2,1,0:T(8,128)(2,1)S(1)} %get-tuple-element.107), channel_id=1, source_target_pairs={{0,3},{1,0},{2,1},{3,2},{4,7},{5,4},{6,5},{7,6},{8,11},{9,8},{10,9... | collective-permute-start | bytes 393224 | tf_op jit(solution)/shard_map/ppermute | solution.py:316
  75.6 5.2 %collective-permute-start.25 = (bf16[2,6,8,512]{3,2,1,0:T(8,128)(2,1)S(1)}, bf16[2,6,8,512]{3,2,1,0:T(8,128)(2,1)S(1)}, u32[]{:S(2)}, u32[]{:S(2)}) collective-permute-start(bf16[2,6,8,512]{3,2,1,0:T(8,128)(2,1)S(1)} %get-tuple-element.110), channel_id=1, source_target_pairs={{0,16},{16,32},{32,48},{48,64},{64,80},{80,96},{96,112},{112,128},... | collective-permute-start | bytes 294920 | tf_op jit(solution)/shard_map/ppermute | solution.py:316
  78.5 4.3 %collective-permute-start.26 = (bf16[2,6,8,512]{3,2,1,0:T(8,128)(2,1)S(1)}, bf16[2,6,8,512]{3,2,1,0:T(8,128)(2,1)S(1)}, u32[]{:S(2)}, u32[]{:S(2)}) collective-permute-start(bf16[2,6,8,512]{3,2,1,0:T(8,128)(2,1)S(1)} %get-tuple-element.111), channel_id=1, source_target_pairs={{0,240},{16,0},{32,16},{48,32},{64,48},{80,64},{96,80},{112,96},{1... | collective-permute-start | bytes 294920 | tf_op jit(solution)/shard_map/ppermute | solution.py:316
  83.1 5.1 %collective-permute-start.27 = (bf16[2,8,8,512]{3,2,1,0:T(8,128)(2,1)S(1)}, bf16[2,8,8,512]{3,2,1,0:T(8,128)(2,1)S(1)}, u32[]{:S(2)}, u32[]{:S(2)}) collective-permute-start(bf16[2,8,8,512]{3,2,1,0:T(8,128)(2,1)S(1)} %get-tuple-element.116), channel_id=1, source_target_pairs={{0,1},{1,2},{2,3},{3,0},{4,5},{5,6},{6,7},{7,4},{8,9},{9,10},{10,1... | collective-permute-start | bytes 393224 | tf_op jit(solution)/shard_map/ppermute | solution.py:316
  83.2 5.0 %collective-permute-start.28 = (bf16[2,8,8,512]{3,2,1,0:T(8,128)(2,1)S(1)}, bf16[2,8,8,512]{3,2,1,0:T(8,128)(2,1)S(1)}, u32[]{:S(2)}, u32[]{:S(2)}) collective-permute-start(bf16[2,8,8,512]{3,2,1,0:T(8,128)(2,1)S(1)} %get-tuple-element.117), channel_id=1, source_target_pairs={{0,3},{1,0},{2,1},{3,2},{4,7},{5,4},{6,5},{7,6},{8,11},{9,8},{10,9... | collective-permute-start | bytes 393224 | tf_op jit(solution)/shard_map/ppermute | solution.py:316
  88.2 3.9 %collective-permute-start.29 = (bf16[2,6,8,512]{3,2,1,0:T(8,128)(2,1)S(1)}, bf16[2,6,8,512]{3,2,1,0:T(8,128)(2,1)S(1)}, u32[]{:S(2)}, u32[]{:S(2)}) collective-permute-start(bf16[2,6,8,512]{3,2,1,0:T(8,128)(2,1)S(1)} %get-tuple-element.120), channel_id=1, source_target_pairs={{0,16},{16,32},{32,48},{48,64},{64,80},{80,96},{96,112},{112,128},... | collective-permute-start | bytes 294920 | tf_op jit(solution)/shard_map/ppermute | solution.py:316
  89.5 4.0 %collective-permute-start.30 = (bf16[2,6,8,512]{3,2,1,0:T(8,128)(2,1)S(1)}, bf16[2,6,8,512]{3,2,1,0:T(8,128)(2,1)S(1)}, u32[]{:S(2)}, u32[]{:S(2)}) collective-permute-start(bf16[2,6,8,512]{3,2,1,0:T(8,128)(2,1)S(1)} %get-tuple-element.121), channel_id=1, source_target_pairs={{0,240},{16,0},{32,16},{48,32},{64,48},{80,64},{96,80},{112,96},{1... | collective-permute-start | bytes 294920 | tf_op jit(solution)/shard_map/ppermute | solution.py:316
  124.8 0.5 copy-start.5
